TPU v7x, 128 devices: a whole 4x4x4 slice. The times are simulated.
128 devices in a mesh: rows: 32 (over x, z, core), modes: 4 (over y).
Axes of the slice: x: 4, y: 4, z: 4, core: 2. Of those that a mesh axis runs over, the one named last changes fastest.
Arguments:
- activations: bfloat16 [2048, 64, 2048], P('rows', None, 'modes'), may hold values from -6 to 6
- cotangent: bfloat16 [2048, 64, 2048], P('rows', None, 'modes'), may hold values from -6 to 6
- spectral_weight: bfloat16 [64, 64, 64, 128], P('rows', None, None, 'modes'), may hold values from -12 to 12
- linear_weight: bfloat16 [64, 64], replicated, may hold values from -0.75 to 0.75
- bias: float32 [64], replicated, may hold values from -4 to 4
Outputs:
- grad_input: bfloat16 [2048, 64, 2048], P('rows', None, 'modes')
- grad_spectral: float32 [64, 64, 64, 128], P('rows', None, None, 'modes')
- grad_linear: float32 [64, 64], replicated
- grad_bias: float32 [64], replicated
All inputs are finite; a program needn't handle non-finite values.
Results may differ from a plain program's by a relative error of at most 0.03.
Values may be sent and summed in bfloat16 or wider, within the bound.
A program may use at most 128 MiB of HBM per device.

v0:
```python
import math

import jax
import jax.numpy as jnp
from jax import lax
from jax.sharding import PartitionSpec as P

HIGHEST_PRECISION = lax.Precision.HIGHEST


def row_angles(freq_count, row_start, row_count, period):
    positions = jnp.arange(freq_count, dtype=jnp.int32)
    frequency = jnp.where(positions < freq_count // 2, positions, positions - freq_count)
    grid_rows = row_start + jnp.arange(row_count, dtype=jnp.int32)
    phases = frequency[:, None] * grid_rows[None, :] % period
    angles = phases.astype(jnp.float32) * (2.0 * math.pi / period)
    return (jnp.cos(angles), jnp.sin(angles))


def column_table(mode_count, col_start, col_count, period):
    mode_ids = jnp.arange(mode_count, dtype=jnp.int32)
    grid_cols = col_start + jnp.arange(col_count, dtype=jnp.int32)
    phases = grid_cols[:, None] * mode_ids[None, :] % period
    angles = phases.astype(jnp.float32) * (2.0 * math.pi / period)
    return jnp.stack([jnp.cos(angles), -jnp.sin(angles)], axis=-1).reshape(
        col_count, 2 * mode_count
    )


def column_weights(mode_count):
    mode_ids = jnp.arange(mode_count, dtype=jnp.int32)
    return jnp.repeat(jnp.where(mode_ids == 0, 1.0, 2.0).astype(jnp.float32), 2)


def to_freq(values, cos_rows, sin_rows):
    length = cos_rows.shape[0]
    stacked = jnp.concatenate([cos_rows, sin_rows], axis=0)
    product = jnp.dot(
        stacked,
        values.reshape(values.shape[0], -1),
        precision=HIGHEST_PRECISION,
        preferred_element_type=jnp.float32,
    )
    halves = product.reshape(2, length, values.shape[1], values.shape[2] // 2, 2)
    real_part = halves[0, ..., 0] + halves[1, ..., 1]
    imag_part = halves[0, ..., 1] - halves[1, ..., 0]
    return jnp.stack([real_part, imag_part], axis=-1).reshape(
        length, values.shape[1], values.shape[2]
    )


def to_rows(values, cos_cols, sin_cols):
    length = cos_cols.shape[0]
    stacked = jnp.concatenate([cos_cols, sin_cols], axis=0)
    product = jnp.dot(
        stacked, values.reshape(values.shape[0], -1), preferred_element_type=jnp.float32
    )
    halves = product.reshape(2, length, values.shape[1], values.shape[2] // 2, 2)
    real_part = halves[0, ..., 0] - halves[1, ..., 1]
    imag_part = halves[0, ..., 1] + halves[1, ..., 0]
    return jnp.stack([real_part, imag_part], axis=-1).reshape(
        length, values.shape[1], values.shape[2]
    )


def gelu_grad(preact):
    cumulative = 0.5 * (1.0 + jax.scipy.special.erf(preact * 0.7071067811865476))
    density = jnp.exp(-0.5 * preact * preact) * 0.3989422804014327
    return cumulative + preact * density


def body(activations, cotangent, spectral_weight, linear_weight, bias):
    rows_here, channels, cols_here = activations.shape
    row_devices = lax.axis_size("rows")
    mode_devices = lax.axis_size("modes")
    row_index = lax.axis_index("rows")
    mode_index = lax.axis_index("modes")
    grid_rows = rows_here * row_devices
    grid_cols = cols_here * mode_devices
    kept_rows = spectral_weight.shape[0]
    block_cols = spectral_weight.shape[3]
    freq_rows = kept_rows * row_devices
    spec_cols = block_cols * mode_devices
    inv_area = 1.0 / (grid_rows * grid_cols)
    forward_table = column_table(spec_cols // 2, mode_index * cols_here, cols_here, grid_cols)
    analysis = forward_table.astype(jnp.bfloat16)
    synthesis = (forward_table.T * column_weights(spec_cols // 2)[:, None]).astype(jnp.bfloat16)
    cos_rows, sin_rows = row_angles(freq_rows, row_index * rows_here, rows_here, grid_rows)
    cos_cols = cos_rows.T.astype(jnp.bfloat16)
    sin_cols = sin_rows.T.astype(jnp.bfloat16)

    def reduce_spectrum(term):
        arranged = term.reshape(row_devices, kept_rows, channels, mode_devices, block_cols)
        arranged = arranged.transpose(0, 3, 1, 2, 4).reshape(
            row_devices * mode_devices * kept_rows, channels, block_cols
        )
        return lax.psum_scatter(arranged, ("rows", "modes"), scatter_dimension=0, tiled=True)

    def expand_spectrum(spectrum):
        gathered = lax.all_gather(spectrum, ("rows", "modes"), axis=0, tiled=True)
        arranged = gathered.reshape(row_devices, mode_devices, kept_rows, channels, block_cols)
        arranged = arranged.transpose(0, 2, 3, 1, 4).reshape(freq_rows, channels, spec_cols)
        return to_rows(arranged, cos_cols, sin_cols).astype(jnp.bfloat16)

    partial_cols = jnp.einsum(
        "hcw,wq->hcq", activations, analysis, preferred_element_type=jnp.float32
    )
    spectrum = reduce_spectrum(to_freq(partial_cols, cos_rows, sin_rows)).astype(jnp.bfloat16)
    parts = spectrum.reshape(kept_rows, channels, block_cols // 2, 2)
    wparts = spectral_weight.reshape(kept_rows, channels, channels, block_cols // 2, 2)
    spec_re = parts[..., 0]
    spec_im = parts[..., 1]
    weight_re = wparts[..., 0]
    weight_im = wparts[..., 1]
    mixed_re = jnp.einsum(
        "kcm,kcom->kom", spec_re, weight_re, preferred_element_type=jnp.float32
    ) - jnp.einsum("kcm,kcom->kom", spec_im, weight_im, preferred_element_type=jnp.float32)
    mixed_im = jnp.einsum(
        "kcm,kcom->kom", spec_re, weight_im, preferred_element_type=jnp.float32
    ) + jnp.einsum("kcm,kcom->kom", spec_im, weight_re, preferred_element_type=jnp.float32)
    mixed = (
        jnp.stack([mixed_re, mixed_im], axis=-1)
        .reshape(kept_rows, channels, block_cols)
        .astype(jnp.bfloat16)
    )
    rowfield = expand_spectrum(mixed)
    spectral = (
        jnp.einsum("hcq,qw->hcw", rowfield, synthesis, preferred_element_type=jnp.float32)
        * inv_area
    )
    linear = jnp.einsum(
        "hcw,co->how", activations, linear_weight, preferred_element_type=jnp.float32
    )
    preact = spectral + linear + bias[None, :, None]
    dpre = (cotangent.astype(jnp.float32) * gelu_grad(preact)).astype(jnp.bfloat16)
    grad_lin_part = jnp.einsum("hcw,how->co", activations, dpre, preferred_element_type=jnp.float32)
    grad_bias_part = jnp.sum(dpre.astype(jnp.float32), axis=(0, 2))
    grad_lin_sum, grad_bias_sum = lax.psum((grad_lin_part, grad_bias_part), ("rows", "modes"))
    dpartial = (
        jnp.einsum("hcw,qw->hcq", dpre, synthesis, preferred_element_type=jnp.float32) * inv_area
    )
    dmixed = reduce_spectrum(to_freq(dpartial, cos_rows, sin_rows)).astype(jnp.bfloat16)
    dparts = dmixed.reshape(kept_rows, channels, block_cols // 2, 2)
    dmix_re = dparts[..., 0]
    dmix_im = dparts[..., 1]
    spec_re_wide = spec_re.astype(jnp.float32)
    spec_im_wide = spec_im.astype(jnp.float32)
    dmix_re_wide = dmix_re.astype(jnp.float32)
    dmix_im_wide = dmix_im.astype(jnp.float32)
    grad_real = (
        spec_re_wide[:, :, None, :] * dmix_re_wide[:, None, :, :]
        + spec_im_wide[:, :, None, :] * dmix_im_wide[:, None, :, :]
    )
    grad_imag = (
        spec_re_wide[:, :, None, :] * dmix_im_wide[:, None, :, :]
        - spec_im_wide[:, :, None, :] * dmix_re_wide[:, None, :, :]
    )
    grad_spectral = jnp.stack([grad_real, grad_imag], axis=-1).reshape(
        kept_rows, channels, channels, block_cols
    )
    dspec_re = jnp.einsum(
        "kcom,kom->kcm", weight_re, dmix_re, preferred_element_type=jnp.float32
    ) + jnp.einsum("kcom,kom->kcm", weight_im, dmix_im, preferred_element_type=jnp.float32)
    dspec_im = jnp.einsum(
        "kcom,kom->kcm", weight_re, dmix_im, preferred_element_type=jnp.float32
    ) - jnp.einsum("kcom,kom->kcm", weight_im, dmix_re, preferred_element_type=jnp.float32)
    dspectrum = (
        jnp.stack([dspec_re, dspec_im], axis=-1)
        .reshape(kept_rows, channels, block_cols)
        .astype(jnp.bfloat16)
    )
    drows = expand_spectrum(dspectrum)
    spectral_part = jnp.einsum("hcq,wq->hcw", drows, analysis, preferred_element_type=jnp.float32)
    local_part = jnp.einsum("how,co->hcw", dpre, linear_weight, preferred_element_type=jnp.float32)
    grad_input = (spectral_part + local_part).astype(jnp.bfloat16)
    return (grad_input, grad_spectral, grad_lin_sum / grid_rows, grad_bias_sum / grid_rows)


def solution(mesh):
    return jax.shard_map(
        body,
        mesh=mesh,
        in_specs=(
            P("rows", None, "modes"),
            P("rows", None, "modes"),
            P("rows", None, None, "modes"),
            P(),
            P(),
        ),
        out_specs=(P("rows", None, "modes"), P("rows", None, None, "modes"), P(), P()),
        check_vma=False,
    )
```

profile of v0, /device:TPU:0, one launch (start us, length us, event | category | flops | bytes accessed | tf_op | source)
XLA Modules:
  0.0 1560.1 jit_solution(16695946387777610892)
XLA Ops:
  7.3 0.5 fusion.58
  7.8 0.6 copy-done.3
  9.0 3.4 convolution_bitcast_fusion
  12.4 2.8 copy.152
  15.2 0.3 fusion.71
  15.6 0.6 copy-done.8
  16.2 14.0 fusion.10
  30.2 0.6 fusion.23
  30.7 0.6 fusion.25
  31.3 2.5 pad_maximum_fusion
  33.8 7.2 copy.98
  41.0 4.9 copy.99
  46.0 1.1 copy-done.5
  47.2 0.4 copy.100
  47.6 645.7 %reduce-scatter.3.cloned.1.call-done = f32[2,64,32]{1,2,0:T(8,128)} async-done(((f32[256,64,32]{1,2,0:T(8,128)}), f32[2,64,32]{1,2,0:T(8,128)}) %reduce-scatter.3.cloned.1.call-update) | async-done | bytes 16400 | tf_op jit(solution)/shard_map/reduce_scatter | solution.py:97
  693.3 0.8 convert_element_type.104
  695.1 0.6 copy.103
  696.0 0.7 mul.222
  696.7 0.6 pad_maximum_fusion.7
  697.3 59.4 %all-gather.3.cloned.1.call-done = bf16[256,64,32]{1,2,0:T(8,128)(2,1)} async-done(((bf16[2,64,32]{1,2,0:T(8,128)(2,1)}), bf16[256,64,32]{1,2,0:T(8,128)(2,1)}) %all-gather.3.cloned.1.call-update) | async-done | bytes 1048592 | tf_op jit(solution)/shard_map/all_gather | solution.py:100
  756.7 6.9 copy.104
  763.6 5.9 reshape_reshape.13
  769.5 1.1 copy.105
  770.6 2.9 fusion.28
  773.5 0.5 fusion.35
  774.0 0.5 fusion.36
  774.4 0.5 pad_maximum_fusion.2
  774.9 3.7 copy.109
  778.7 4.3 fusion.32
  783.0 6.0 convert_reduce_fusion
  789.1 2.0 copy-done.1
  791.1 1.3 convolution_multiply_fusion
  792.4 2.7 copy.158
  795.1 14.1 fusion.8
  809.3 0.6 fusion.17
  809.8 0.6 fusion.19
  810.4 2.4 pad_maximum_fusion.1
  812.8 7.3 copy.118
  820.2 4.8 copy.119
  825.1 0.6 copy-done.12
  825.9 4.8 convolution_bitcast_fusion.1
  830.7 64.6 %all-reduce = (f32[64,64]{0,1:T(8,128)S(1)}, f32[64]{0:T(128)S(1)}) all-reduce(f32[64,64]{0,1:T(8,128)S(1)} %convolution_bitcast_fusion.1, f32[64]{0:T(128)S(1)} %get-tuple-element.34), channel_id=1, replica_groups=mesh['rows'=32,'modes'=4] {'rows','modes'}, use_global_device_ids=true, to_apply=%region_2.3 | all-reduce | flops 4160 | bytes 33280 | tf_op jit(solution)/shard_map/psum | solution.py:138
  895.3 0.7 copy.129
  896.0 571.7 %reduce-scatter.5.cloned.1.call-done = f32[2,64,32]{1,2,0:T(8,128)} async-done(((f32[256,64,32]{1,2,0:T(8,128)}), f32[2,64,32]{1,2,0:T(8,128)}) %reduce-scatter.5.cloned.1.call-update) | async-done | bytes 16400 | tf_op jit(solution)/shard_map/reduce_scatter | solution.py:97
  1467.7 0.8 convert_element_type.109
  1468.4 0.4 fusion.43
  1468.8 0.4 fusion.39
  1469.2 0.4 fusion.44
  1469.6 0.4 fusion.40
  1470.0 0.6 copy.120
  1470.7 0.5 broadcast_multiply_fusion.1
  1471.2 6.7 fusion.67
  1477.9 5.0 multiply_add_fusion
  1482.9 3.6 pad_maximum_fusion.4
  1486.5 43.7 %all-gather.5.cloned.1.call-done = bf16[256,64,32]{1,2,0:T(8,128)(2,1)} async-done(((bf16[2,64,32]{1,2,0:T(8,128)(2,1)}), bf16[256,64,32]{1,2,0:T(8,128)(2,1)}) %all-gather.5.cloned.1.call-update) | async-done | bytes 1048592 | tf_op jit(solution)/shard_map/all_gather | solution.py:100
  1530.2 6.9 copy.121
  1537.1 5.9 reshape_reshape.15
  1543.1 1.4 copy.122
  1544.4 2.3 fusion.26
  1546.8 0.5 fusion.37
  1547.2 0.5 fusion.38
  1547.7 0.5 pad_maximum_fusion.3
  1548.2 0.7 slice-done.1
  1549.0 4.1 fusion.6
  (67 shorter events, 2.5 us)
Async XLA Ops:
  7.2 775.8 %copy-start = (bf16[64,64]{1,0:T(8,128)(2,1)S(1)}, bf16[64,64]{1,0:T(8,128)(2,1)}, u32[]{:S(2)}) copy-start(bf16[64,64]{1,0:T(8,128)(2,1)} %param.8) | copy-start | bytes 24580
  7.2 686.1 %reduce-scatter.3.cloned.1.call-start = ((), (), s32[]{:S(2)}) async-start(), calls=%async_computation.2 | async-start | bytes 4227072 | tf_op jit(solution)/shard_map/reduce_scatter | solution.py:97
  7.8 0.6 copy-start.3
  15.6 0.6 copy-start.8
  45.9 1.2 copy-start.5
  46.0 710.8 %all-gather.3.cloned.1.call-start = ((), (), s32[]{:S(2)}) async-start(), calls=%async_computation.3 | async-start | bytes 2113536 | tf_op jit(solution)/shard_map/all_gather | solution.py:100
  47.6 716.1 %copy-start.6 = (bf16[2,64,64,32]{2,1,3,0:T(8,128)(2,1)}, bf16[2,64,64,32]{2,1,3,0:T(8,128)(2,1)S(1)}, u32[]{:S(2)}) copy-start(bf16[2,64,64,32]{2,1,3,0:T(8,128)(2,1)S(1)} %copy.100) | copy-start | bytes 1572868
  694.1 69.6 %copy-start.11 = (bf16[2,64,32]{1,2,0:T(8,128)(2,1)}, bf16[2,64,32]{1,2,0:T(8,128)(2,1)S(1)}, u32[]{:S(2)}) copy-start(bf16[2,64,32]{1,2,0:T(8,128)(2,1)S(1)} %convert_element_type.104) | copy-start | bytes 24580
  695.7 771.9 %reduce-scatter.5.cloned.1.call-start = ((), (), s32[]{:S(2)}) async-start(), calls=%async_computation.4 | async-start | bytes 4227072 | tf_op jit(solution)/shard_map/reduce_scatter | solution.py:97
  774.4 4.2 copy-start.13
  778.6 4.3 copy-start.2
  778.7 4.4 copy-start.14
  778.7 4.4 copy-start.15
  789.1 2.0 copy-start.1
  792.4 2.7 copy-start.9
  825.0 0.7 copy-start.12
  825.0 705.2 %all-gather.5.cloned.1.call-start = ((), (), s32[]{:S(2)}) async-start(), calls=%async_computation.5 | async-start | bytes 2113536 | tf_op jit(solution)/shard_map/all_gather | solution.py:100
  825.9 642.5 %copy-start.7 = (bf16[2,64,64,32]{2,1,3,0:T(8,128)(2,1)S(1)}, bf16[2,64,64,32]{2,1,3,0:T(8,128)(2,1)}, u32[]{:S(2)}) copy-start(bf16[2,64,64,32]{2,1,3,0:T(8,128)(2,1)} %copy-done.6) | copy-start | bytes 1572868
  1537.1 7.3 copy-start.10
  1544.4 3.8 slice-start
  1546.7 2.2 slice-start.1
  1547.2 1.8 copy-start.4
Sparse Core Ops, SparseCore 0:
  46.1 647.1 reduce-scatter.2
  697.3 59.3 all-gather.2
  825.1 642.5 reduce-scatter.4
  1470.8 59.3 all-gather.4
where the time goes:
time: 1570 us; the launch traced here: 1560 us
  waiting for transfers between devices  1320 us (84%)
  local copies, waits for them, and re-layouts  71.3 us (5%)
  matrix products  66.4 us (4%)
  blocking collectives  64.6 us (4%)
  other arithmetic  22.1 us (1%)
    reduce_scatter x2, waiting for transfers between devices, reduce_spectrum(): lax.psum_scatter(arranged, ('rows', 'modes'), scatter_dimension=0, tiled=...  1220 us
    all_gather x2, waiting for transfers between devices, expand_spectrum(): gathered = lax.all_gather(spectrum, ('rows', 'modes'), axis=0, tiled=True)  103 us
    psum x1, blocking collectives, body(): lax.psum((grad_lin_part, grad_bias_part), ('rows', 'modes'))  64.6 us
  transfers between devices with their start and end apart: 4, of which 4 were waited for; matrix products, arithmetic and copies ran while one was open for 1% of the time, Pallas kernels for 0%

commit v1 on v0

v1 whole, which is shorter than its diff:
```python
import functools
import math

import jax
import jax.numpy as jnp
import numpy as np
from jax import lax
from jax.experimental import pallas as pl
from jax.experimental.pallas import tpu as pltpu
from jax.sharding import PartitionSpec as P

MESH = pl.DeviceIdType.MESH
BF = jnp.bfloat16
F32 = jnp.float32
VMEM = pl.BlockSpec(memory_space=pltpu.VMEM)
LIMIT = 60 * 1024 * 1024


def dot(a, b):
    return jnp.dot(a, b, preferred_element_type=F32)


def lanes_of(shape):
    return lax.broadcasted_iota(jnp.int32, shape, len(shape) - 1)


def row_table(row_index):
    slot = jnp.arange(64, dtype=jnp.int32)
    core, z, x, jj = slot // 32, (slot // 8) % 4, (slot // 2) % 4, slot % 2
    mode = x * 16 + z * 4 + core * 2 + jj
    freq = jnp.where(mode < 32, mode, mode - 64)
    rows = row_index * 64 + jnp.arange(64, dtype=jnp.int32)
    ang = (freq[:, None] * rows[None, :] % 2048).astype(F32) * (2.0 * math.pi / 2048)
    return jnp.cos(ang), jnp.sin(ang)


def col_tables(mode_index):
    q = jnp.arange(128, dtype=jnp.int32)
    cols = mode_index * 512 + jnp.arange(512, dtype=jnp.int32)
    ang = ((cols[:, None] * (q // 2)[None, :]) % 2048).astype(F32) * (2.0 * math.pi / 2048)
    even = (q % 2 == 0)[None, :]
    c, s = jnp.cos(ang), jnp.sin(ang)
    ana = jnp.where(even, c, -s).astype(BF)
    swap = jnp.where(even, -s, -c).astype(BF)
    return ana, swap


def kron8(c, s):
    up = (lax.broadcasted_iota(jnp.int32, (512, 64), 0) // 8 == lax.broadcasted_iota(jnp.int32, (512, 64), 1)).astype(BF)
    wide = (lax.broadcasted_iota(jnp.int32, (64, 512), 1) // 8 == lax.broadcasted_iota(jnp.int32, (64, 512), 0)).astype(BF)
    keep = lax.broadcasted_iota(jnp.int32, (512, 512), 0) % 8 == lax.broadcasted_iota(jnp.int32, (512, 512), 1) % 8
    parts = []
    for t in (c, s):
        parts.append(jnp.where(keep, dot(dot(up, t).astype(BF), wide), 0.0).astype(BF))
    return parts


def forward(field_ref, tab_ref, rmat_ref, tile_ref, out_ref):
    tab = tab_ref[...]
    for a in range(4):
        lhs = field_ref[:, 16 * a : 16 * a + 16, :].reshape(1024, 512)
        p = dot(lhs, tab).reshape(64, 2, 8, 256)
        cols = []
        for g in range(2):
            pg = p[:, g].reshape(512, 256)
            cols.append(jnp.concatenate([pg[:, :128], pg[:, 128:]], axis=0).astype(BF))
        o = dot(rmat_ref[...], jnp.concatenate(cols, axis=1))
        for g in range(2):
            tile_ref[a, :, 8 * g : 8 * g + 8, :] = o[:, 128 * g : 128 * g + 128].reshape(64, 8, 128)
    for m in range(4):
        exchange(lambda a: tile_ref[a].reshape(1024, 128), m, lambda v: store_mode(out_ref, m, v))


def store_mode(out_ref, m, v):
    v = v.reshape(2, 4, 4, 2, 16, 128).astype(BF)
    for core in range(2):
        out_ref[core, m] = v[core]


def exchange(get, m, put):
    block = lanes_of((1024, 128)) // 32
    total = None
    for a in range(4):
        v = get(a)
        shift = (32 * (a - m)) % 128
        if shift:
            v = pltpu.roll(v, shift, 1)
        total = v if total is None else jnp.where(block == a, v, total)
    put(total)


def inverse(g_ref, imat_ref, out_ref):
    even = lanes_of((1024, 128)) % 2 == 0
    for b in range(4):
        def build(v, b=b):
            swapped = jnp.where(even, -pltpu.roll(v, 127, 1), pltpu.roll(v, 1, 1))
            v3, s3 = v.reshape(64, 16, 128), swapped.reshape(64, 16, 128)
            cols = []
            for g in range(2):
                cols.append(
                    jnp.concatenate(
                        [v3[:, 8 * g : 8 * g + 8].reshape(512, 128), s3[:, 8 * g : 8 * g + 8].reshape(512, 128)], axis=0
                    ).astype(BF)
                )
            o = dot(imat_ref[...], jnp.concatenate(cols, axis=1))
            both = jnp.concatenate([o[:, :128].reshape(64, 8, 128), o[:, 128:].reshape(64, 8, 128)], axis=1)
            out_ref[:, 16 * b : 16 * b + 16, :] = both.astype(BF)

        def get(m):
            parts = [g_ref[core, m].reshape(512, 128) for core in range(2)]
            return jnp.concatenate(parts, axis=0).astype(F32)

        exchange(get, b, build)


def gelu_grad(z):
    e = jnp.exp(-0.5 * z * z)
    az = jnp.abs(z)
    t = 1.0 / (1.0 + (0.3275911 * 0.7071067811865476) * az)
    poly = t * (0.5 * 0.254829592 + t * (-0.5 * 0.284496736 + t * (0.5 * 1.421413741 + t * (-0.5 * 1.453152027 + t * (0.5 * 1.061405429)))))
    tail = poly * e
    return jnp.where(z >= 0, 1.0 - tail, tail) + (0.3989422804014327 * z) * e


def first_kernel(act_ref, tab_ref, crow_ref, srow_ref, crow_t_ref, srow_t_ref, out_ref, rmat_ref, imat_ref, tile_ref):
    c, s = kron8(crow_ref[...], srow_ref[...])
    rmat_ref[:, :512] = c
    rmat_ref[:, 512:] = s
    c, s = kron8(crow_t_ref[...], srow_t_ref[...])
    imat_ref[:, :512] = c
    imat_ref[:, 512:] = s
    forward(act_ref, tab_ref, rmat_ref, tile_ref, out_ref)


def middle_kernel(g_ref, act_ref, cot_ref, rmat_ref, imat_ref, syn_ref, lw_t_ref, bias_ref, tab_ref,
                  dpre_ref, out_ref, lin_ref, rf_ref, tile_ref):
    inverse(g_ref, imat_ref, rf_ref)
    lin_ref[...] = jnp.zeros_like(lin_ref)
    bias = bias_ref[...]

    def row(h, _):
        lhs = jnp.concatenate([rf_ref[h], lw_t_ref[...]], axis=1)
        rhs = jnp.concatenate([syn_ref[...], act_ref[h]], axis=0)
        pre = dot(lhs, rhs) + bias
        d = (cot_ref[h].astype(F32) * gelu_grad(pre)).astype(BF)
        dpre_ref[h] = d
        both = jnp.concatenate([act_ref[h], jnp.ones((16, 512), BF)], axis=0)
        lin_ref[...] += lax.dot_general(both, d, (((1,), (1,)), ((), ())), preferred_element_type=F32)
        return 0

    lax.fori_loop(0, 64, row, 0)
    forward(dpre_ref, tab_ref, rmat_ref, tile_ref, out_ref)


def last_kernel(g_ref, dpre_ref, imat_ref, ana_ref, lw_ref, s_ref, d_ref, gin_ref, gspec_ref, rf_ref):
    inverse(g_ref, imat_ref, rf_ref)

    def row(h, _):
        lhs = jnp.concatenate([rf_ref[h], lw_ref[...]], axis=1)
        rhs = jnp.concatenate([ana_ref[...], dpre_ref[h]], axis=0)
        gin_ref[h] = dot(lhs, rhs).astype(BF)
        return 0

    lax.fori_loop(0, 64, row, 0)
    for jj in range(2):
        re, im = duplicate(s_ref[jj])
        d = d_ref[jj]
        even = lax.broadcasted_iota(jnp.int32, (32, 64), 0) % 2 == 0
        dsw = jnp.where(even, pltpu.roll(d, 31, 0), -pltpu.roll(d, 1, 0))
        for c in range(64):
            gspec_ref[jj, c] = re[:, c : c + 1] * d + im[:, c : c + 1] * dsw


def duplicate(v):
    even = lax.broadcasted_iota(jnp.int32, v.shape, 0) % 2 == 0
    return jnp.where(even, v, pltpu.roll(v, 1, 0)), jnp.where(even, pltpu.roll(v, v.shape[0] - 1, 0), v)


def to_columns(block):
    rows = [block if a == 0 else pltpu.roll(block, (128 - 32 * a) % 128, 1) for a in range(4)]
    stacked = jnp.concatenate(rows + rows, axis=0)
    return stacked.T[:32, :64]


def to_block(cols):
    wide = jnp.concatenate([cols, cols], axis=1)
    square = jnp.concatenate([wide] * 4, axis=0).T
    out = None
    block = lanes_of((16, 128)) // 32
    for a in range(4):
        v = square[16 * a : 16 * a + 16, :]
        out = v if out is None else jnp.where(block == a, v, out)
    return out


def weigh(s, w_ref, jj):
    re, im = duplicate(s)
    t1 = jnp.zeros((32, 64), F32)
    t2 = jnp.zeros((32, 64), F32)
    for c in range(64):
        w = w_ref[jj, c].astype(F32)
        t1 += re[:, c : c + 1] * w
        t2 += im[:, c : c + 1] * w
    even = lax.broadcasted_iota(jnp.int32, (32, 64), 0) % 2 == 0
    return t1 + jnp.where(even, -pltpu.roll(t2, 31, 0), pltpu.roll(t2, 1, 0))


def weigh_back(d, w_ref, jj):
    even = lax.broadcasted_iota(jnp.int32, (32, 64), 0) % 2 == 0
    dsw = jnp.where(even, pltpu.roll(d, 31, 0), pltpu.roll(d, 1, 0))
    lane = lanes_of((32, 64))
    u1 = jnp.zeros((32, 64), F32)
    u2 = jnp.zeros((32, 64), F32)
    for c in range(64):
        w = w_ref[jj, c].astype(F32)
        u1 = jnp.where(lane == c, jnp.sum(w * d, axis=1, keepdims=True), u1)
        u2 = jnp.where(lane == c, jnp.sum(w * dsw, axis=1, keepdims=True), u2)
    return jnp.where(even, u1 + pltpu.roll(u1, 31, 0), pltpu.roll(u2, 1, 0) - u2)


def place():
    r, y = lax.axis_index("rows"), lax.axis_index("modes")
    return r // 8, y, (r // 2) % 4, r % 2


def device(x, y, z, core):
    return ((x * 4 + z) * 2 + core, y)


def greet():
    x, y, z, core = place()
    barrier = pltpu.get_barrier_semaphore()
    peers = [device(x, y, z, 1 - core)]
    for d in range(1, 4):
        peers += [device((x + d) % 4, y, z, core), device(x, (y + d) % 4, z, core), device(x, y, (z + d) % 4, core)]
    for p in peers:
        pl.semaphore_signal(barrier, inc=1, device_id=p, device_id_type=MESH)
    pl.semaphore_wait(barrier, len(peers))


def remote(src, dst, send, recv, target):
    return pltpu.make_async_remote_copy(src_ref=src, dst_ref=dst, send_sem=send, recv_sem=recv, device_id=target, device_id_type=MESH)


def reduce_scatter(t_ref, b0, a1, b1, a2, b2, a3, b3, send, recv):
    x, y, z, core = place()
    pending = []
    first = []
    for i, d in enumerate((1, 2, 3, 0)):
        yt = (y + d) % 4
        cp = remote(t_ref.at[1 - core, yt], b0.at[yt], send.at[i], recv.at[i], device(x, y, z, 1 - core))
        cp.start()
        first.append(cp)
    pending += first
    stage = []
    for i, d in enumerate((1, 2, 3, 0)):
        yt = (y + d) % 4
        first[i].wait_recv()
        a1[yt] = (t_ref[core, yt].astype(F32) + b0[yt].astype(F32)).astype(BF)
        if d:
            cp = remote(a1.at[yt], b1.at[d - 1], send.at[3 + d], recv.at[3 + d], device(x, yt, z, core))
            cp.start()
            stage.append(cp)
    for cp in stage:
        cp.wait_recv()
    pending += stage
    stage = []
    for d in (1, 2, 3, 0):
        zt = (z + d) % 4
        v = a1[y, zt].astype(F32)
        for k in range(3):
            v += b1[k, zt].astype(F32)
        a2[zt] = v.astype(BF)
        if d:
            cp = remote(a2.at[zt], b2.at[d - 1], send.at[6 + d], recv.at[6 + d], device(x, y, zt, core))
            cp.start()
            stage.append(cp)
    for cp in stage:
        cp.wait_recv()
    pending += stage
    stage = []
    for d in (1, 2, 3, 0):
        xt = (x + d) % 4
        v = a2[z, xt].astype(F32)
        for k in range(3):
            v += b2[k, xt].astype(F32)
        a3[xt] = v.astype(BF)
        if d:
            cp = remote(a3.at[xt], b3.at[d - 1], send.at[9 + d], recv.at[9 + d], device(xt, y, z, core))
            cp.start()
            stage.append(cp)
        else:
            own = v
    for cp in stage:
        cp.wait_recv()
    pending += stage
    for k in range(3):
        own += b3[k].astype(F32)
    for cp in pending:
        cp.wait_send()
    return own


def all_gather(g_ref, send, recv):
    x, y, z, core = place()
    pending = []

    def stage(base, target, source, mine, theirs):
        cps = []
        for d in range(1, 4):
            out = remote(mine, mine, send.at[base + d], recv.at[base + d], target(d))
            out.start()
            cps.append(out)
        pending.extend(cps)
        return [remote(theirs(d), theirs(d), send.at[base + d], recv.at[base + d], source(d)) for d in range(1, 4)]

    for cp in stage(-1, lambda d: device((x + d) % 4, y, z, core), lambda d: device((x - d) % 4, y, z, core),
                    g_ref.at[core, y, z, x], lambda d: g_ref.at[core, y, z, (x + 4 - d) % 4]):
        cp.wait_recv()
    for cp in stage(2, lambda d: device(x, y, (z + d) % 4, core), lambda d: device(x, y, (z - d) % 4, core),
                    g_ref.at[core, y, z], lambda d: g_ref.at[core, y, (z + 4 - d) % 4]):
        cp.wait_recv()
    waits = stage(5, lambda d: device(x, (y + d) % 4, z, core), lambda d: device(x, (y - d) % 4, z, core),
                  g_ref.at[core, y], lambda d: g_ref.at[core, (y + 4 - d) % 4])
    last = []
    for d in range(4):
        ys = (y + 4 - d) % 4
        if d:
            waits[d - 1].wait_recv()
        cp = remote(g_ref.at[core, ys], g_ref.at[core, ys], send.at[9 + d], recv.at[9 + d], device(x, y, z, 1 - core))
        cp.start()
        last.append(cp)
    for d in range(4):
        ys = (y + 4 - d) % 4
        remote(g_ref.at[1 - core, ys], g_ref.at[1 - core, ys], send.at[9 + d], recv.at[9 + d], device(x, y, z, 1 - core)).wait_recv()
    for cp in pending + last:
        cp.wait_send()


def forward_exchange(t_ref, w_ref, s_ref, g_ref, b0, a1, b1, a2, b2, a3, b3, send, recv, send2, recv2):
    x, y, z, core = place()
    greet()
    own = reduce_scatter(t_ref, b0, a1, b1, a2, b2, a3, b3, send, recv)
    for jj in range(2):
        s = to_columns(own[jj].astype(BF).astype(F32))
        s_ref[jj] = s
        g_ref[core, y, z, x, jj] = to_block(weigh(s, w_ref, jj)).astype(BF)
    all_gather(g_ref, send2, recv2)


def backward_exchange(t_ref, w_ref, lin_ref, d_ref, g_ref, lin_out_ref,
                      b0, a1, b1, a2, b2, a3, b3, part, send, recv, send2, recv2, send3, recv3):
    x, y, z, core = place()
    greet()
    own = reduce_scatter(t_ref, b0, a1, b1, a2, b2, a3, b3, send, recv)
    for jj in range(2):
        d = to_columns(own[jj].astype(BF).astype(F32))
        d_ref[jj] = d
        g_ref[core, y, z, x, jj] = to_block(weigh_back(d, w_ref, jj)).astype(BF)
    all_gather(g_ref, send2, recv2)
    part[0, core] = lin_ref[...]
    cp = remote(part.at[0, core], part.at[0, core], send3.at[0], recv3.at[0], device(x, y, z, 1 - core))
    cp.start()
    remote(part.at[0, 1 - core], part.at[0, 1 - core], send3.at[0], recv3.at[0], device(x, y, z, 1 - core)).wait_recv()
    cp.wait_send()
    v = part[0, 0] + part[0, 1]
    for i, (me, at) in enumerate(((y, lambda p: device(x, p, z, core)), (z, lambda p: device(x, y, p, core)), (x, lambda p: device(p, y, z, core)))):
        part[i + 1, me] = v
        cps = []
        for d in range(1, 4):
            cp = remote(part.at[i + 1, me], part.at[i + 1, me], send3.at[3 * i + d], recv3.at[3 * i + d], at((me + d) % 4))
            cp.start()
            cps.append(cp)
        for d in range(1, 4):
            src = (me + 4 - d) % 4
            remote(part.at[i + 1, src], part.at[i + 1, src], send3.at[3 * i + d], recv3.at[3 * i + d], at(src)).wait_recv()
        for cp in cps:
            cp.wait_send()
        v = part[i + 1, 0] + part[i + 1, 1] + part[i + 1, 2] + part[i + 1, 3]
    lin_out_ref[...] = v * (1.0 / 2048)


def exchange_scratch():
    dma = pltpu.SemaphoreType.DMA
    return [
        pltpu.VMEM((4, 4, 4, 2, 16, 128), BF),
        pltpu.VMEM((4, 4, 4, 2, 16, 128), BF),
        pltpu.VMEM((3, 4, 4, 2, 16, 128), BF),
        pltpu.VMEM((4, 4, 2, 16, 128), BF),
        pltpu.VMEM((3, 4, 2, 16, 128), BF),
        pltpu.VMEM((4, 2, 16, 128), BF),
        pltpu.VMEM((3, 2, 16, 128), BF),
    ], [dma((13,))] * 4


def call(kernel, outs, scratch, args, collective=None):
    params = dict(vmem_limit_bytes=LIMIT)
    if collective is not None:
        params.update(collective_id=collective, has_side_effects=True)
    return pl.pallas_call(
        kernel,
        out_shape=[jax.ShapeDtypeStruct(s, t) for s, t in outs],
        in_specs=[VMEM] * len(args),
        out_specs=[VMEM] * len(outs),
        scratch_shapes=scratch,
        compiler_params=pltpu.CompilerParams(**params),
    )(*args)


SPEC = (2, 4, 4, 4, 2, 16, 128)


def body(activations, cotangent, spectral_weight, linear_weight, bias):
    row_index, mode_index = lax.axis_index("rows"), lax.axis_index("modes")
    crow, srow = row_table(row_index)
    crow, srow = crow.astype(BF), srow.astype(BF)
    ana, swap = col_tables(mode_index)
    tab = jnp.concatenate([ana, swap], axis=1)
    weights = jnp.where(jnp.arange(128) < 2, 1.0, 2.0).astype(BF) * BF(2.0**-22)
    dtab = tab * jnp.concatenate([weights, weights])[None, :]
    syn = (ana * weights[None, :]).T
    w = spectral_weight.transpose(0, 1, 3, 2)

    tile = pltpu.VMEM((4, 64, 16, 128), F32)
    t, rmat, imat = call(
        first_kernel, [(SPEC, BF), ((512, 1024), BF), ((512, 1024), BF)], [tile],
        [activations, tab, crow, srow, crow.T, srow.T],
    )
    buffers, sems = exchange_scratch()
    s, g = call(forward_exchange, [((2, 32, 64), F32), (SPEC, BF)], buffers + sems, [t, w], 0)
    dpre, t, lin = call(
        middle_kernel, [((64, 64, 512), BF), (SPEC, BF), ((80, 64), F32)],
        [pltpu.VMEM((64, 64, 128), BF), tile],
        [g, activations, cotangent, rmat, imat, syn, linear_weight.T, bias[:, None], dtab],
    )
    d, g, lin = call(
        backward_exchange, [((2, 32, 64), F32), (SPEC, BF), ((80, 64), F32)],
        buffers + [pltpu.VMEM((4, 4, 80, 64), F32)] + sems + [pltpu.SemaphoreType.DMA((10,))] * 2, [t, w, lin], 1,
    )
    gin, gspec = call(
        last_kernel, [((64, 64, 512), BF), ((2, 64, 32, 64), F32)], [pltpu.VMEM((64, 64, 128), BF)],
        [g, dpre, imat, ana.T, linear_weight, s, d],
    )
    return gin, gspec.transpose(0, 1, 3, 2), lin[:64], lin[64]


def solution(mesh):
    return jax.shard_map(
        body,
        mesh=mesh,
        in_specs=(
            P("rows", None, "modes"),
            P("rows", None, "modes"),
            P("rows", None, None, "modes"),
            P(),
            P(),
        ),
        out_specs=(P("rows", None, "modes"), P("rows", None, None, "modes"), P(), P()),
        check_vma=False,
    )
```

time: 1570 us -> 171 us (0.11)
  waiting for transfers between devices: 1320 us -> 0 us
  Pallas kernels: 0 us -> 160 us
  local copies, waits for them, and re-layouts: 71.3 us -> 3.89 us
  matrix products: 66.4 us -> 0 us
  blocking collectives: 64.6 us -> 0 us
    reduce_scatter x2 -> x0, waiting for transfers between devices: 1220 us -> none  [reduce_spectrum(): lax.psum_scatter(arranged, ('rows', 'modes'), scatter_dimension=0, tiled=...]
    pallas_call x0 -> x5, Pallas kernels: none -> 160 us  [call(): pl.pallas_call(kernel, out_shape=[jax.ShapeDtypeStruct(s, t) for s, t in...]
    all_gather x2 -> x0, waiting for transfers between devices: 103 us -> none  [expand_spectrum(): gathered = lax.all_gather(spectrum, ('rows', 'modes'), axis=0, tiled=True)]
    dot_general x19 -> x0, matrix products: 66.4 us -> none  [the longest x2 28.1 us: to_freq(): jnp.dot(stacked, values.reshape(values.shape[0], -1), precision=HIGHEST_P...]
    psum x1 -> x0, blocking collectives: 64.6 us -> none  [body(): lax.psum((grad_lin_part, grad_bias_part), ('rows', 'modes'))]
    another operation x8 -> x0, local copies, waits for them, and re-layouts: 31.5 us -> none  [the longest x2 14.5 us: to_freq(): jnp.stack([real_part, imag_part], axis=-1)]
    reshape x6 -> x0, local copies, waits for them, and re-layouts: 19.7 us -> none  [the longest x2 13.8 us: expand_spectrum(): gathered.reshape(row_devices, mode_devices, kept_rows, channels, block_cols)]
  transfers between devices with their start and end apart: 4 -> 0, of which waited for: 4 -> 0; matrix products, arithmetic and copies ran while one was open for 1% -> 0% of each run, Pallas kernels for 0% -> 0%
where the time goes in v1:
time: 171 us
  Pallas kernels  160 us (94%)
  other arithmetic  6.88 us (4%)
  local copies, waits for them, and re-layouts  3.89 us (2%)
    pallas_call x5, Pallas kernels, call(): pl.pallas_call(kernel, out_shape=[jax.ShapeDtypeStruct(s, t) for s, t in...  160 us

profile of v1, /device:TPU:0, one launch (start us, length us, event | category | flops | bytes accessed | tf_op | source)
XLA Modules:
  0.0 171.1 jit_solution(602785440779104985)
XLA Ops:
  0.7 1.4 copy.9
  2.1 1.4 copy.10.bias_ref
  3.5 1.0 sine_convert_fusion
  4.4 1.9 %broadcast_multiply_fusion.1.syn_ref = bf16[128,512]{1,0:T(8,128)(2,1)} fusion(bf16[128]{0:T(256)(128)(2,1)S(1)} %fusion.20, s32[128]{0:T(128)S(1)} %and_select_fusion.6, s32[512]{0:T(512)S(1)} %iota_add_fusion, pred[128]{0:T(512)(128)(4,1)S(1)} %fusion.14), kind=kLoop, calls=%fused_computation.23 | loop fusion | flops 1376256 | bytes 134016 | tf_op jit(solution)/shard_map/mul | solution.py:421
  6.3 1.8 %select_convert_fusion.ana_ref = bf16[128,512]{1,0:T(8,128)(2,1)} fusion(s32[128]{0:T(128)S(1)} %and_select_fusion.6, s32[512]{0:T(512)S(1)} %iota_add_fusion, pred[128]{0:T(512)(128)(4,1)S(1)} %fusion.14), kind=kLoop, calls=%fused_computation.17 | loop fusion | flops 1114112 | bytes 133760 | tf_op jit(solution)/shard_map/convert_element_type | solution.py:43
  8.2 1.3 select_convert_fusion.2
  9.4 0.9 broadcast_multiply_fusion
  10.3 7.5 %shard_map.84 = (bf16[2,4,4,4,2,16,128]{6,5,4,3,2,1,0:T(8,128)(2,1)}, bf16[512,1024]{1,0:T(8,128)(2,1)}, bf16[512,1024]{1,0:T(8,128)(2,1)}) custom-call(bf16[64,64,512]{2,1,0:T(8,128)(2,1)} %act_ref.3, bf16[512,256]{1,0:T(8,128)(2,1)} %get-tuple-element.31.tab_ref, bf16[64,64]{1,0:T(8,128)(2,1)} %get-tuple-element.37.crow_ref, ...), custom_call_target="tpu_custom_call" | custom-call | tf_op jit(solution)/shard_map/pallas_call | solution.py:400
  17.8 42.2 %shard_map.85 = (f32[2,32,64]{2,1,0:T(8,128)}, bf16[2,4,4,4,2,16,128]{6,5,4,3,2,1,0:T(8,128)(2,1)}) custom-call(bf16[2,4,4,4,2,16,128]{6,5,4,3,2,1,0:T(8,128)(2,1)} %get-tuple-element.17.t_ref, bf16[2,64,32,64]{3,2,1,0:T(8,128)(2,1)} %bitcast.6), custom_call_target="tpu_custom_call" | custom-call | tf_op jit(solution)/shard_map/pallas_call | solution.py:400
  60.0 38.6 %shard_map.86 = (bf16[64,64,512]{2,1,0:T(8,128)(2,1)}, bf16[2,4,4,4,2,16,128]{6,5,4,3,2,1,0:T(8,128)(2,1)}, f32[80,64]{1,0:T(8,128)}) custom-call(bf16[2,4,4,4,2,16,128]{6,5,4,3,2,1,0:T(8,128)(2,1)} %get-tuple-element.18.g_ref, bf16[64,64,512]{2,1,0:T(8,128)(2,1)} %act_ref.3, bf16[64,64,512]{2,1,0:T(8,128)(2,1)} %cot_ref.1, ...), custom_call_target="tpu_custom_call" | custom-call | tf_op jit(solution)/shard_map/pallas_call | solution.py:400
  98.5 53.6 %shard_map.87 = (f32[2,32,64]{2,1,0:T(8,128)}, bf16[2,4,4,4,2,16,128]{6,5,4,3,2,1,0:T(8,128)(2,1)}, f32[80,64]{1,0:T(8,128)}) custom-call(bf16[2,4,4,4,2,16,128]{6,5,4,3,2,1,0:T(8,128)(2,1)} %get-tuple-element.21.t_ref, bf16[2,64,32,64]{3,2,1,0:T(8,128)(2,1)} %bitcast.7, f32[80,64]{1,0:T(8,128)} %get-tuple-element.22.lin_ref), custom_call_target="tpu_custom_call" | custom-call | tf_op jit(solution)/shard_map/pallas_call | solution.py:400
  152.1 0.0 copy-start
  152.1 17.8 %shard_map.88 = (bf16[64,64,512]{2,1,0:T(8,128)(2,1)}, f32[2,64,32,64]{3,2,1,0:T(8,128)}) custom-call(bf16[2,4,4,4,2,16,128]{6,5,4,3,2,1,0:T(8,128)(2,1)} %get-tuple-element.23.g_ref, bf16[64,64,512]{2,1,0:T(8,128)(2,1)} %get-tuple-element.24.dpre_ref, bf16[512,1024]{1,0:T(8,128)(2,1)} %get-tuple-element.20.imat_ref, ...), custom_call_target="tpu_custom_call" | custom-call | tf_op jit(solution)/shard_map/pallas_call | solution.py:400
  169.9 0.0 copy-done
  169.9 0.5 slice_bitcast_fusion
  170.4 0.6 slice.6
  (6 shorter events, 0.0 us)
Async XLA Ops:
  152.1 17.8 %copy-start = (f32[80,64]{1,0:T(8,128)S(1)}, f32[80,64]{1,0:T(8,128)}, u32[]{:S(2)}) copy-start(f32[80,64]{1,0:T(8,128)} %get-tuple-element.29) | copy-start | bytes 61444

commit v2 on v0

v2 whole, which is shorter than its diff:
```python
import math

import jax
import jax.numpy as jnp
import numpy as np
from jax import lax
from jax.experimental import pallas as pl
from jax.experimental.pallas import tpu as pltpu
from jax.sharding import PartitionSpec as P

MESH = pl.DeviceIdType.MESH
BF = jnp.bfloat16
F32 = jnp.float32
VMEM = pl.BlockSpec(memory_space=pltpu.VMEM)
LIMIT = 60 * 1024 * 1024


def dot(a, b):
    return jnp.dot(a, b, preferred_element_type=F32)


def lanes_of(shape):
    return lax.broadcasted_iota(jnp.int32, shape, len(shape) - 1)


def column_constants():
    k = np.arange(128) // 2
    w = np.arange(2048)
    ang = ((w[:, None] * k[None, :]) % 2048) * (2.0 * math.pi / 2048)
    even = (np.arange(128) % 2 == 0)[None, :]
    ana = np.where(even, np.cos(ang), -np.sin(ang))
    swap = np.where(even, -np.sin(ang), -np.cos(ang))
    return np.concatenate([ana, swap], axis=1).reshape(4, 512, 256).astype(np.float32).astype(jnp.bfloat16)


def row_constants():
    slot = np.arange(64)
    core, z, x, jj = slot // 32, (slot // 8) % 4, (slot // 2) % 4, slot % 2
    mode = x * 16 + z * 4 + core * 2 + jj
    freq = np.where(mode < 32, mode, mode - 64)
    rows = np.arange(2048).reshape(32, 64)
    ang = ((freq[None, :, None] * rows[:, None, :]) % 2048) * (2.0 * math.pi / 2048)
    return np.stack([np.cos(ang), np.sin(ang)], axis=1).astype(np.float32).astype(jnp.bfloat16)


def kron8(table, flip):
    up = (lax.broadcasted_iota(jnp.int32, (512, 64), 0) // 8 == lax.broadcasted_iota(jnp.int32, (512, 64), 1)).astype(BF)
    wide = (lax.broadcasted_iota(jnp.int32, (64, 512), 1) // 8 == lax.broadcasted_iota(jnp.int32, (64, 512), 0)).astype(BF)
    keep = lax.broadcasted_iota(jnp.int32, (512, 512), 0) % 8 == lax.broadcasted_iota(jnp.int32, (512, 512), 1) % 8
    left = lax.dot_general(up, table, (((1,), (1 if flip else 0,)), ((), ())), preferred_element_type=F32).astype(BF)
    return jnp.where(keep, dot(left, wide), 0.0).astype(BF)


def place():
    r, y = lax.axis_index("rows"), lax.axis_index("modes")
    x, z, core = r // 8, (r // 2) % 4, r % 2
    return y * (1 - core) + z * core, z * (1 - core) + y * core, x, core


def device(p, q, x, core):
    y, z = p * (1 - core) + q * core, q * (1 - core) + p * core
    return ((x * 4 + z) * 2 + core, y)


def sibling(p, q, x, core):
    return device(q, p, x, 1 - core)


def signal_peers():
    p, q, x, core = place()
    barrier = pltpu.get_barrier_semaphore()
    pl.semaphore_signal(barrier, inc=1, device_id=sibling(p, q, x, core), device_id_type=MESH)
    for d in range(1, 4):
        pl.semaphore_signal(barrier, inc=1, device_id=device((p + d) % 4, q, x, core), device_id_type=MESH)
    for k in range(1, 16):
        pl.semaphore_signal(barrier, inc=1, device_id=device(p, (q + k // 4) % 4, (x + k % 4) % 4, core), device_id_type=MESH)


def wait_peers():
    pl.semaphore_wait(pltpu.get_barrier_semaphore(), 19)


def remote(src, dst, send, recv, target):
    return pltpu.make_async_remote_copy(src_ref=src, dst_ref=dst, send_sem=send, recv_sem=recv, device_id=target, device_id_type=MESH)


def columns(block, tab, xs_ref, h0, count):
    prod = dot(block.reshape(count * 64, 512), tab).reshape(count, 8, 8, 256)
    for a in range(4):
        for g in range(2):
            v = prod[:, 2 * a + g].reshape(count * 8, 256).astype(BF)
            xs_ref[g, pl.ds(h0 * 8, count * 8), 128 * a : 128 * a + 128] = v[:, :128]
            xs_ref[g, pl.ds(512 + h0 * 8, count * 8), 128 * a : 128 * a + 128] = v[:, 128:]


def row_modes(xs_ref, rmat_ref, t_ref, owner):
    block = lanes_of((256, 128)) // 32
    for g in range(2):
        o = dot(rmat_ref[pl.ds(pl.multiple_of(owner * 256, 256), 256), :], xs_ref[g])
        for m in range(4):
            total = None
            for a in range(4):
                v = o[:, 128 * a : 128 * a + 128]
                shift = (32 * (a - m)) % 128
                if shift:
                    v = pltpu.roll(v, shift, 1)
                total = v if total is None else jnp.where(block == a, v, total)
            total = total.astype(BF).reshape(4, 4, 16, 128)
            for z in range(4):
                t_ref[owner, m * (1 - owner) + z * owner, z * (1 - owner) + m * owner, :, g] = total[z]


def inverse(g_ref, imat_ref, out_ref):
    even = lanes_of((512, 128)) % 2 == 0
    block = lanes_of((512, 128)) // 32
    for b in range(4):
        cols = []
        for g in range(2):
            total = None
            for m in range(4):
                parts = [g_ref[0, m, :, :, g].reshape(256, 128)]
                parts += [g_ref[1, z, m, :, g].reshape(64, 128) for z in range(4)]
                v = jnp.concatenate(parts, axis=0).astype(F32)
                shift = (32 * (m - b)) % 128
                if shift:
                    v = pltpu.roll(v, shift, 1)
                total = v if total is None else jnp.where(block == m, v, total)
            swapped = jnp.where(even, -pltpu.roll(total, 127, 1), pltpu.roll(total, 1, 1))
            cols.append(jnp.concatenate([total.astype(BF), swapped.astype(BF)], axis=0))
        o = dot(imat_ref[...], jnp.concatenate(cols, axis=1))
        both = jnp.concatenate([o[:, :128].reshape(64, 8, 128), o[:, 128:].reshape(64, 8, 128)], axis=1)
        out_ref[:, 16 * b : 16 * b + 16, :] = both.astype(BF)


def gelu_grad(z):
    e = jnp.exp(-0.5 * z * z)
    t = 1.0 / (1.0 + (0.3275911 * 0.7071067811865476) * jnp.abs(z))
    poly = t * (0.5 * 0.254829592 + t * (-0.5 * 0.284496736 + t * (0.5 * 1.421413741 + t * (-0.5 * 1.453152027 + t * (0.5 * 1.061405429)))))
    tail = poly * e
    return jnp.where(z >= 0, 1.0 - tail, tail) + (0.3989422804014327 * z) * e


def duplicate(v):
    even = lax.broadcasted_iota(jnp.int32, v.shape, 0) % 2 == 0
    return jnp.where(even, v, pltpu.roll(v, 1, 0)), jnp.where(even, pltpu.roll(v, v.shape[0] - 1, 0), v)


def to_columns(block):
    turned = [[block[g] if a == 0 else pltpu.roll(block[g], 128 - 32 * a, 1) for g in range(2)] for a in range(4)]
    out = []
    for jj in range(2):
        rows = [turned[a][g][8 * jj : 8 * jj + 8] for a in range(4) for g in range(2)]
        out.append(jnp.concatenate(rows + rows, axis=0).T[:32, :64])
    return out


def to_block(cols):
    block = lanes_of((8, 128)) // 32
    parts = []
    for v in cols:
        square = jnp.concatenate([jnp.concatenate([v, v], axis=1)] * 4, axis=0).T
        parts.append([])
        for g in range(2):
            out = square[8 * g : 8 * g + 8]
            for a in range(1, 4):
                out = jnp.where(block == a, square[16 * a + 8 * g : 16 * a + 8 * g + 8], out)
            parts[-1].append(out)
    return [jnp.concatenate([parts[0][g], parts[1][g]], axis=0) for g in range(2)]


def weigh(s, w_ref, jj):
    re, im = duplicate(s)
    t1 = jnp.zeros((32, 64), F32)
    t2 = jnp.zeros((32, 64), F32)
    for c in range(64):
        w = w_ref[jj, c].astype(F32)
        t1 += re[:, c : c + 1] * w
        t2 += im[:, c : c + 1] * w
    even = lax.broadcasted_iota(jnp.int32, (32, 64), 0) % 2 == 0
    return t1 + jnp.where(even, -pltpu.roll(t2, 31, 0), pltpu.roll(t2, 1, 0))


def weigh_back(d, w_ref, jj):
    even = lax.broadcasted_iota(jnp.int32, (32, 64), 0) % 2 == 0
    dsw = jnp.where(even, pltpu.roll(d, 31, 0), pltpu.roll(d, 1, 0))
    lane = lanes_of((32, 64))
    u1 = jnp.zeros((32, 64), F32)
    u2 = jnp.zeros((32, 64), F32)
    for c in range(64):
        w = w_ref[jj, c].astype(F32)
        u1 = jnp.where(lane == c, jnp.sum(w * d, axis=1, keepdims=True), u1)
        u2 = jnp.where(lane == c, jnp.sum(w * dsw, axis=1, keepdims=True), u2)
    return jnp.where(even, u1 + pltpu.roll(u1, 31, 0), pltpu.roll(u2, 1, 0) - u2)


def start_core(t_ref, b0, send, recv):
    p, q, x, core = place()
    cps = []
    for d in (1, 2, 3, 0):
        cp = remote(t_ref.at[1 - core, (q + d) % 4], b0.at[(q + d) % 4], send.at[d], recv.at[d], sibling(p, q, x, core))
        cp.start()
        cps.append(cp)
    return cps


def reduce_scatter(t_ref, bufs, send, recv, between=lambda i: None):
    b0, a1, b1, a2, b2 = bufs
    p, q, x, core = place()
    pending = []
    for d in (1, 2, 3, 0):
        pt = (p + d) % 4
        remote(b0.at[pt], b0.at[pt], send.at[d], recv.at[d], sibling(p, q, x, core)).wait_recv()
        a1[pt] = (t_ref[core, pt].astype(F32) + b0[pt].astype(F32)).astype(BF)
        if d:
            cp = remote(a1.at[pt], b1.at[d - 1], send.at[3 + d], recv.at[3 + d], device(pt, q, x, core))
            cp.start()
            pending.append(cp)
    between(0)
    for cp in pending:
        cp.wait_recv()
    a2[...] = (a1[p].astype(F32) + b1[0].astype(F32) + b1[1].astype(F32) + b1[2].astype(F32)).astype(BF)
    stage = []
    for k in range(1, 16):
        qt, xt = (q + k // 4) % 4, (x + k % 4) % 4
        cp = remote(a2.at[qt, xt], b2.at[k - 1], send.at[6 + k], recv.at[6 + k], device(p, qt, xt, core))
        cp.start()
        stage.append(cp)
    own = a1[p, q, x].astype(F32)
    for k in range(3):
        own += b1[k, q, x].astype(F32)
    between(1)
    for cp in stage:
        cp.wait_recv()
    for k in range(15):
        own += b2[k].astype(F32)
    for d in range(4):
        remote(t_ref.at[1 - core, (q + d) % 4], b0.at[(q + d) % 4], send.at[d], recv.at[d], sibling(p, q, x, core)).wait_send()
    for cp in pending + stage:
        cp.wait_send()
    return own


def all_gather(g_ref, send, recv, between=lambda i: None):
    p, q, x, core = place()
    pending = []
    mine = g_ref.at[core, p, q, x]
    for k in range(1, 16):
        cp = remote(mine, mine, send.at[6 + k], recv.at[6 + k], device(p, (q + k // 4) % 4, (x + k % 4) % 4, core))
        cp.start()
        pending.append(cp)
    between(2)
    for k in range(1, 16):
        qs, xs = (q + 4 - k // 4) % 4, (x + 4 - k % 4) % 4
        theirs = g_ref.at[core, p, qs, xs]
        remote(theirs, theirs, send.at[6 + k], recv.at[6 + k], device(p, qs, xs, core)).wait_recv()
    mine = g_ref.at[core, p]
    for d in range(1, 4):
        cp = remote(mine, mine, send.at[3 + d], recv.at[3 + d], device((p + d) % 4, q, x, core))
        cp.start()
        pending.append(cp)
    between(3)
    for d in range(4):
        ps = (p + 4 - d) % 4
        theirs = g_ref.at[core, ps]
        if d:
            remote(theirs, theirs, send.at[3 + d], recv.at[3 + d], device(ps, q, x, core)).wait_recv()
        cp = remote(theirs, theirs, send.at[d], recv.at[d], sibling(p, q, x, core))
        cp.start()
        pending.append(cp)
    between(4)
    for d in range(4):
        theirs = g_ref.at[1 - core, (q + 4 - d) % 4]
        remote(theirs, theirs, send.at[d], recv.at[d], sibling(p, q, x, core)).wait_recv()
    for cp in pending:
        cp.wait_send()


def main_kernel(act_hbm, cot_hbm, w_hbm, coltab_hbm, rowtab_hbm, lw_ref, bias_ref,
                dpre_hbm, s_ref, d_ref, g2_ref, lin_out_ref, imat_ref,
                act, cot, w_ref, tab, dtab, syn, rowtab, rmat, lw_t, xs, rf, dpre, lin, t1, t2, g1, part,
                b0, a1, b1, a2, b2, c0, e1, c1, e2, c2,
                in_sem, out_sem, send1, recv1, send2, recv2, send3, recv3, send4, recv4, send5, recv5):
    p, q, x, core = place()
    signal_peers()
    row_dev, mode_dev = lax.axis_index("rows"), lax.axis_index("modes")
    loads = [
        pltpu.make_async_copy(coltab_hbm.at[mode_dev], tab, in_sem.at[0]),
        pltpu.make_async_copy(rowtab_hbm.at[row_dev], rowtab, in_sem.at[1]),
    ]
    loads += [pltpu.make_async_copy(act_hbm.at[pl.ds(16 * i, 16)], act.at[pl.ds(16 * i, 16)], in_sem.at[2 + i]) for i in range(4)]
    loads.append(pltpu.make_async_copy(w_hbm, w_ref, in_sem.at[6]))
    loads.append(pltpu.make_async_copy(cot_hbm, cot, in_sem.at[7]))
    for cp in loads:
        cp.start()
    loads[1].wait()
    rmat[:, :512] = kron8(rowtab[0], False)
    rmat[:, 512:] = kron8(rowtab[1], False)
    loads[0].wait()
    for i in range(4):
        loads[2 + i].wait()
        columns(act[16 * i : 16 * i + 16], tab[...], xs, 16 * i, 16)
    row_modes(xs, rmat, t1, 1 - core)
    wait_peers()
    start_core(t1, b0, send1, recv1)
    row_modes(xs, rmat, t1, core)

    def prepare(i):
        if i == 0:
            imat_ref[:, :512] = kron8(rowtab[0], True)
            imat_ref[:, 512:] = kron8(rowtab[1], True)
            lw_t[...] = lw_ref[...].astype(F32).T.astype(BF)
        if i == 1:
            lane = lanes_of((512, 256)) % 128
            scaled = tab[...].astype(F32) * jnp.where(lane < 2, 2.0**-22, 2.0**-21)
            dtab[...] = scaled.astype(BF)
            syn[...] = scaled[:, :128].T.astype(BF)

    own = reduce_scatter(t1, (b0, a1, b1, a2, b2), send1, recv1, prepare)
    loads[6].wait()
    s = to_columns(own.astype(BF).astype(F32))
    mixed = []
    for jj in range(2):
        s_ref[jj] = s[jj]
        mixed.append(weigh(s[jj], w_ref, jj))
    for g, v in enumerate(to_block(mixed)):
        g1[core, p, q, x, g] = v.astype(BF)
    all_gather(g1, send2, recv2)

    inverse(g1, imat_ref, rf)
    loads[7].wait()
    bias = bias_ref[...]

    def rows(i, _):
        for n in range(2):
            ds = []
            for k in range(2):
                h = 4 * i + 2 * n + k
                lhs = jnp.concatenate([rf[h], lw_t[...]], axis=1)
                rhs = jnp.concatenate([syn[...], act[h]], axis=0)
                d = (cot[h].astype(F32) * gelu_grad(dot(lhs, rhs) + bias)).astype(BF)
                dpre[h] = d
                ds.append(d)
            columns(jnp.concatenate(ds, axis=0).reshape(2, 64, 512), dtab[...], xs, pl.multiple_of(4 * i + 2 * n, 2), 2)
        return 0

    stores = []
    for i in range(4):
        lax.fori_loop(4 * i, 4 * i + 4, rows, 0)
        cp = pltpu.make_async_copy(dpre.at[pl.ds(16 * i, 16)], dpre_hbm.at[pl.ds(16 * i, 16)], out_sem.at[i])
        cp.start()
        stores.append(cp)

    row_modes(xs, rmat, t2, 1 - core)
    start_core(t2, c0, send3, recv3)
    row_modes(xs, rmat, t2, core)

    steps = ((p, lambda v: device(v, q, x, core)), (q, lambda v: device(p, v, x, core)), (x, lambda v: device(p, q, v, core)))

    def swap_lin():
        part[0, core] = lin[...]
        remote(part.at[0, core], part.at[0, core], send5.at[0], recv5.at[0], sibling(p, q, x, core)).start()

    def join_lin(i):
        if i == 0:
            cp = remote(part.at[0, core], part.at[0, core], send5.at[0], recv5.at[0], sibling(p, q, x, core))
            cp.wait_send()
            remote(part.at[0, 1 - core], part.at[0, 1 - core], send5.at[0], recv5.at[0], sibling(p, q, x, core)).wait_recv()
            return part[0, 0] + part[0, 1]
        me, at = steps[i - 1]
        for d in range(1, 4):
            src = (me + 4 - d) % 4
            remote(part.at[i, src], part.at[i, src], send5.at[3 * i - 3 + d], recv5.at[3 * i - 3 + d], at(src)).wait_recv()
            remote(part.at[i, me], part.at[i, me], send5.at[3 * i - 3 + d], recv5.at[3 * i - 3 + d], at((me + d) % 4)).wait_send()
        return part[i, 0] + part[i, 1] + part[i, 2] + part[i, 3]

    def pass_lin(i):
        me, at = steps[i]
        part[i + 1, me] = join_lin(i)
        for d in range(1, 4):
            remote(part.at[i + 1, me], part.at[i + 1, me], send5.at[3 * i + d], recv5.at[3 * i + d], at((me + d) % 4)).start()

    def products(i, _):
        left = jnp.concatenate([act[4 * i + k] for k in range(4)], axis=1)
        right = jnp.concatenate([dpre[4 * i + k] for k in range(4)], axis=1)
        left = jnp.concatenate([left, jnp.ones((16, 2048), BF)], axis=0)
        lin[...] += lax.dot_general(left, right, (((1,), (1,)), ((), ())), preferred_element_type=F32)
        return 0

    def local_products(i):
        if i == 0:
            lin[...] = jnp.zeros_like(lin)
            lax.fori_loop(0, 16, products, 0)
            swap_lin()
        if i >= 2:
            pass_lin(i - 2)

    own = reduce_scatter(t2, (c0, e1, c1, e2, c2), send3, recv3, local_products)
    d = to_columns(own.astype(BF).astype(F32))
    back = []
    for jj in range(2):
        d_ref[jj] = d[jj]
        back.append(weigh_back(d[jj], w_ref, jj))
    for g, v in enumerate(to_block(back)):
        g2_ref[core, p, q, x, g] = v.astype(BF)
    all_gather(g2_ref, send4, recv4, local_products)
    lin_out_ref[...] = join_lin(3) * (1.0 / 2048)
    for cp in stores:
        cp.wait()


def last_kernel(g_ref, dpre_ref, imat_ref, coltab_hbm, lw_ref, s_ref, d_ref, gin_ref, gspec_ref, rf_ref, tab, ana, sem):
    load = pltpu.make_async_copy(coltab_hbm.at[lax.axis_index("modes")], tab, sem)
    load.start()
    inverse(g_ref, imat_ref, rf_ref)
    load.wait()
    ana[...] = tab[:, :128].astype(F32).T.astype(BF)

    def row(h, _):
        for k in range(4):
            lhs = jnp.concatenate([rf_ref[4 * h + k], lw_ref[...]], axis=1)
            rhs = jnp.concatenate([ana[...], dpre_ref[4 * h + k]], axis=0)
            gin_ref[4 * h + k] = dot(lhs, rhs).astype(BF)
        return 0

    lax.fori_loop(0, 16, row, 0)
    for jj in range(2):
        re, im = duplicate(s_ref[jj])
        d = d_ref[jj]
        even = lax.broadcasted_iota(jnp.int32, (32, 64), 0) % 2 == 0
        dsw = jnp.where(even, pltpu.roll(d, 31, 0), -pltpu.roll(d, 1, 0))
        for c in range(64):
            gspec_ref[jj, c] = re[:, c : c + 1] * d + im[:, c : c + 1] * dsw


SPEC = (2, 4, 4, 4, 2, 16, 128)
ANY = pl.BlockSpec(memory_space=pl.ANY)


def body(activations, cotangent, spectral_weight, linear_weight, bias):
    w = spectral_weight.transpose(0, 1, 3, 2)
    coltab, rowtab = jnp.asarray(column_constants()), jnp.asarray(row_constants())
    dma = pltpu.SemaphoreType.DMA
    quarter = (4, 4, 4, 2, 16, 128)
    buffers = [pltpu.VMEM(quarter, BF), pltpu.VMEM(quarter, BF), pltpu.VMEM((3, 4, 4, 2, 16, 128), BF),
               pltpu.VMEM((4, 4, 2, 16, 128), BF), pltpu.VMEM((15, 2, 16, 128), BF)]
    shape = jax.ShapeDtypeStruct
    dpre, s, d, g, lin, imat = pl.pallas_call(
        main_kernel,
        out_shape=[shape((64, 64, 512), BF), shape((2, 32, 64), F32), shape((2, 32, 64), F32), shape(SPEC, BF),
                   shape((80, 64), F32), shape((512, 1024), BF)],
        in_specs=[ANY] * 5 + [VMEM] * 2,
        out_specs=[ANY] + [VMEM] * 5,
        scratch_shapes=[
            pltpu.VMEM((64, 64, 512), BF), pltpu.VMEM((64, 64, 512), BF), pltpu.VMEM((2, 64, 32, 64), BF),
            pltpu.VMEM((512, 256), BF), pltpu.VMEM((512, 256), BF), pltpu.VMEM((128, 512), BF), pltpu.VMEM((2, 64, 64), BF),
            pltpu.VMEM((512, 1024), BF), pltpu.VMEM((64, 64), BF), pltpu.VMEM((2, 1024, 512), BF),
            pltpu.VMEM((64, 64, 128), BF), pltpu.VMEM((64, 64, 512), BF), pltpu.VMEM((80, 64), F32),
            pltpu.VMEM(SPEC, BF), pltpu.VMEM(SPEC, BF), pltpu.VMEM(SPEC, BF), pltpu.VMEM((4, 4, 80, 64), F32),
        ] + buffers + buffers + [dma((8,)), dma((4,))] + [dma((22,))] * 8 + [dma((10,))] * 2,
        compiler_params=pltpu.CompilerParams(vmem_limit_bytes=LIMIT, collective_id=0, has_side_effects=True),
        name="main",
    )(activations, cotangent, w, coltab, rowtab, linear_weight, bias[:, None])
    gin, gspec = pl.pallas_call(
        last_kernel,
        out_shape=[shape((64, 64, 512), BF), shape((2, 64, 32, 64), F32)],
        in_specs=[VMEM] * 3 + [ANY] + [VMEM] * 3,
        out_specs=[VMEM] * 2,
        scratch_shapes=[pltpu.VMEM((64, 64, 128), BF), pltpu.VMEM((512, 256), BF), pltpu.VMEM((128, 512), BF), dma],
        compiler_params=pltpu.CompilerParams(vmem_limit_bytes=LIMIT),
        name="last",
    )(g, dpre, imat, coltab, linear_weight, s, d)
    return gin, gspec.transpose(0, 1, 3, 2), lin[:64], lin[64]


def solution(mesh):
    return jax.shard_map(
        body,
        mesh=mesh,
        in_specs=(
            P("rows", None, "modes"),
            P("rows", None, "modes"),
            P("rows", None, None, "modes"),
            P(),
            P(),
        ),
        out_specs=(P("rows", None, "modes"), P("rows", None, None, "modes"), P(), P()),
        check_vma=False,
    )
```

time: 1570 us -> 102 us (0.06)
  waiting for transfers between devices: 1320 us -> 0 us
  Pallas kernels: 0 us -> 98.3 us
  local copies, waits for them, and re-layouts: 71.3 us -> 2.49 us
  matrix products: 66.4 us -> 0 us
  blocking collectives: 64.6 us -> 0 us
  other arithmetic: 22.1 us -> 0 us
    reduce_scatter x2 -> x0, waiting for transfers between devices: 1220 us -> none  [reduce_spectrum(): lax.psum_scatter(arranged, ('rows', 'modes'), scatter_dimension=0, tiled=...]
    all_gather x2 -> x0, waiting for transfers between devices: 103 us -> none  [expand_spectrum(): gathered = lax.all_gather(spectrum, ('rows', 'modes'), axis=0, tiled=True)]
    pallas_call x0 -> x2, Pallas kernels: none -> 98.3 us  [the longest x1 86 us: body(): pl.pallas_call(main_kernel, out_shape=[shape((64, 64, 512), BF), shape((2...]
    dot_general x19 -> x0, matrix products: 66.4 us -> none  [the longest x2 28.1 us: to_freq(): jnp.dot(stacked, values.reshape(values.shape[0], -1), precision=HIGHEST_P...]
    psum x1 -> x0, blocking collectives: 64.6 us -> none  [body(): lax.psum((grad_lin_part, grad_bias_part), ('rows', 'modes'))]
    another operation x8 -> x0, local copies, waits for them, and re-layouts: 31.5 us -> none  [the longest x2 14.5 us: to_freq(): jnp.stack([real_part, imag_part], axis=-1)]
    reshape x6 -> x0, local copies, waits for them, and re-layouts: 19.7 us -> none  [the longest x2 13.8 us: expand_spectrum(): gathered.reshape(row_devices, mode_devices, kept_rows, channels, block_cols)]
  transfers between devices with their start and end apart: 4 -> 0, of which waited for: 4 -> 0; matrix products, arithmetic and copies ran while one was open for 1% -> 0% of each run, Pallas kernels for 0% -> 0%
where the time goes in v2:
time: 102 us; the launch traced here: 101 us
  Pallas kernels  98.3 us (96%)
  local copies, waits for them, and re-layouts  2.49 us (2%)
    pallas_call x1, Pallas kernels, body(): pl.pallas_call(main_kernel, out_shape=[shape((64, 64, 512), BF), shape((2...  86 us
    pallas_call x1, Pallas kernels, body(): pl.pallas_call(last_kernel, out_shape=[shape((64, 64, 512), BF), shape((2...  12.3 us

profile of v2, /device:TPU:0, one launch (start us, length us, event | category | flops | bytes accessed | tf_op | source)
XLA Modules:
  0.0 101.5 jit_solution(2409943563591464084)
XLA Ops:
  0.6 1.4 %copy.11.bias_ref = f32[64,1]{1,0:T(8,128)} copy(f32[64,1]{0,1:T(1,128)} %bitcast.6) | data formatting | bytes 512 | tf_op jit(solution)/shard_map/broadcast_in_dim | solution.py:462
  2.0 86.0 %main.1 = (bf16[64,64,512]{2,1,0:T(8,128)(2,1)}, f32[2,32,64]{2,1,0:T(8,128)}, f32[2,32,64]{2,1,0:T(8,128)}, bf16[2,4,4,4,2,16,128]{6,5,4,3,2,1,0:T(8,128)(2,1)}...) custom-call(bf16[64,64,512]{2,1,0:T(8,128)(2,1)} %act_hbm.1, bf16[64,64,512]{2,1,0:T(8,128)(2,1)} %cot_hbm.1, ...), custom_call_target="tpu_custom_call" | custom-call | tf_op jit(solution)/shard_map/main/pallas_call | solution.py:447
  88.0 0.0 copy-start
  88.0 12.3 %last.1 = (bf16[64,64,512]{2,1,0:T(8,128)(2,1)}, f32[2,64,32,64]{3,2,1,0:T(8,128)}) custom-call(bf16[2,4,4,4,2,16,128]{6,5,4,3,2,1,0:T(8,128)(2,1)} %get-tuple-element.12.g_ref, bf16[64,64,512]{2,1,0:T(8,128)(2,1)} %get-tuple-element.13.dpre_ref, bf16[512,1024]{1,0:T(8,128)(2,1)} %get-tuple-element.14.imat_ref, ...), custom_call_target="tpu_custom_call" | custom-call | tf_op jit(solution)/shard_map/last/pallas_call | solution.py:463
  100.3 0.0 copy-done
  100.3 0.5 slice_bitcast_fusion
  100.8 0.6 slice.6
Async XLA Ops:
  88.0 12.3 %copy-start = (f32[80,64]{1,0:T(8,128)S(1)}, f32[80,64]{1,0:T(8,128)}, u32[]{:S(2)}) copy-start(f32[80,64]{1,0:T(8,128)} %get-tuple-element.19) | copy-start | bytes 61444

commit v3 on v2

--- a/solution.py
+++ b/solution.py
@@ -133,11 +133,12 @@
 
 
 def gelu_grad(z):
-    e = jnp.exp(-0.5 * z * z)
-    t = 1.0 / (1.0 + (0.3275911 * 0.7071067811865476) * jnp.abs(z))
+    u = (0.3275911 * 0.7071067811865476) * jnp.abs(z)
+    e = jnp.exp2((-0.5 * 1.4426950408889634) * z * z)
+    t = 1.0 / (1.0 + u)
     poly = t * (0.5 * 0.254829592 + t * (-0.5 * 0.284496736 + t * (0.5 * 1.421413741 + t * (-0.5 * 1.453152027 + t * (0.5 * 1.061405429)))))
-    tail = poly * e
-    return jnp.where(z >= 0, 1.0 - tail, tail) + (0.3989422804014327 * z) * e
+    r = (poly - (0.3989422804014327 / (0.3275911 * 0.7071067811865476)) * u) * e
+    return jnp.where(z >= 0, 1.0 - r, r)
 
 
 def duplicate(v):
@@ -195,12 +196,9 @@
 
 def start_core(t_ref, b0, send, recv):
     p, q, x, core = place()
-    cps = []
     for d in (1, 2, 3, 0):
-        cp = remote(t_ref.at[1 - core, (q + d) % 4], b0.at[(q + d) % 4], send.at[d], recv.at[d], sibling(p, q, x, core))
-        cp.start()
-        cps.append(cp)
-    return cps
+        row = (p + d) % 4
+        remote(t_ref.at[1 - core, :, row], b0.at[:, row], send.at[d], recv.at[d], sibling(p, q, x, core)).start()
 
 
 def reduce_scatter(t_ref, bufs, send, recv, between=lambda i: None):
@@ -208,23 +206,30 @@
     p, q, x, core = place()
     pending = []
     for d in (1, 2, 3, 0):
-        pt = (p + d) % 4
-        remote(b0.at[pt], b0.at[pt], send.at[d], recv.at[d], sibling(p, q, x, core)).wait_recv()
-        a1[pt] = (t_ref[core, pt].astype(F32) + b0[pt].astype(F32)).astype(BF)
-        if d:
-            cp = remote(a1.at[pt], b1.at[d - 1], send.at[3 + d], recv.at[3 + d], device(pt, q, x, core))
-            cp.start()
-            pending.append(cp)
+        row = (q + d) % 4
+        remote(b0.at[:, row], b0.at[:, row], send.at[d], recv.at[d], sibling(p, q, x, core)).wait_recv()
+        for e in (1, 2, 3, 0):
+            pt = (p + e) % 4
+            a1[pt, row] = (t_ref[core, pt, row].astype(F32) + b0[pt, row].astype(F32)).astype(BF)
+            if e:
+                k = 3 + 3 * d + e
+                cp = remote(a1.at[pt, row], b1.at[e - 1, row], send.at[k], recv.at[k], device(pt, q, x, core))
+                cp.start()
+                pending.append(cp)
     between(0)
-    for cp in pending:
-        cp.wait_recv()
-    a2[...] = (a1[p].astype(F32) + b1[0].astype(F32) + b1[1].astype(F32) + b1[2].astype(F32)).astype(BF)
     stage = []
-    for k in range(1, 16):
-        qt, xt = (q + k // 4) % 4, (x + k % 4) % 4
-        cp = remote(a2.at[qt, xt], b2.at[k - 1], send.at[6 + k], recv.at[6 + k], device(p, qt, xt, core))
-        cp.start()
-        stage.append(cp)
+    for i, d in enumerate((1, 2, 3, 0)):
+        row = (q + d) % 4
+        for cp in pending[3 * i : 3 * i + 3]:
+            cp.wait_recv()
+        a2[row] = (a1[p, row].astype(F32) + b1[0, row].astype(F32) + b1[1, row].astype(F32) + b1[2, row].astype(F32)).astype(BF)
+        for n in range(4):
+            k = 4 * d + n
+            if k:
+                xt = (x + n) % 4
+                cp = remote(a2.at[row, xt], b2.at[k - 1], send.at[15 + k], recv.at[15 + k], device(p, row, xt, core))
+                cp.start()
+                stage.append(cp)
     own = a1[p, q, x].astype(F32)
     for k in range(3):
         own += b1[k, q, x].astype(F32)
@@ -234,7 +239,8 @@
     for k in range(15):
         own += b2[k].astype(F32)
     for d in range(4):
-        remote(t_ref.at[1 - core, (q + d) % 4], b0.at[(q + d) % 4], send.at[d], recv.at[d], sibling(p, q, x, core)).wait_send()
+        row = (p + d) % 4
+        remote(t_ref.at[1 - core, :, row], b0.at[:, row], send.at[d], recv.at[d], sibling(p, q, x, core)).wait_send()
     for cp in pending + stage:
         cp.wait_send()
     return own
@@ -244,40 +250,52 @@
     p, q, x, core = place()
     pending = []
     mine = g_ref.at[core, p, q, x]
-    for k in range(1, 16):
-        cp = remote(mine, mine, send.at[6 + k], recv.at[6 + k], device(p, (q + k // 4) % 4, (x + k % 4) % 4, core))
-        cp.start()
-        pending.append(cp)
+    for d in (0, 2, 1, 3):
+        for n in range(4):
+            k = 4 * d + n
+            if k:
+                cp = remote(mine, mine, send.at[15 + k], recv.at[15 + k], device(p, (q + d) % 4, (x + n) % 4, core))
+                cp.start()
+                pending.append(cp)
     between(2)
-    for k in range(1, 16):
-        qs, xs = (q + 4 - k // 4) % 4, (x + 4 - k % 4) % 4
-        theirs = g_ref.at[core, p, qs, xs]
-        remote(theirs, theirs, send.at[6 + k], recv.at[6 + k], device(p, qs, xs, core)).wait_recv()
-    mine = g_ref.at[core, p]
-    for d in range(1, 4):
-        cp = remote(mine, mine, send.at[3 + d], recv.at[3 + d], device((p + d) % 4, q, x, core))
-        cp.start()
-        pending.append(cp)
+    order = (0, 1, 3, 2)
+    for d in order:
+        row = (q + 4 - d) % 4
+        for n in range(4):
+            k = 4 * d + n
+            if k:
+                xs = (x + 4 - n) % 4
+                theirs = g_ref.at[core, p, row, xs]
+                remote(theirs, theirs, send.at[15 + k], recv.at[15 + k], device(p, row, xs, core)).wait_recv()
+        mine = g_ref.at[core, p, row]
+        for e in (1, 2, 3):
+            k = 3 + 3 * d + e
+            cp = remote(mine, mine, send.at[k], recv.at[k], device((p + e) % 4, q, x, core))
+            cp.start()
+            pending.append(cp)
     between(3)
-    for d in range(4):
-        ps = (p + 4 - d) % 4
-        theirs = g_ref.at[core, ps]
-        if d:
-            remote(theirs, theirs, send.at[3 + d], recv.at[3 + d], device(ps, q, x, core)).wait_recv()
+    for d in order:
+        row = (q + 4 - d) % 4
+        for e in (1, 2, 3):
+            k = 3 + 3 * d + e
+            ps = (p + 4 - e) % 4
+            theirs = g_ref.at[core, ps, row]
+            remote(theirs, theirs, send.at[k], recv.at[k], device(ps, q, x, core)).wait_recv()
+        theirs = g_ref.at[core, :, row]
         cp = remote(theirs, theirs, send.at[d], recv.at[d], sibling(p, q, x, core))
         cp.start()
         pending.append(cp)
     between(4)
-    for d in range(4):
-        theirs = g_ref.at[1 - core, (q + 4 - d) % 4]
+    for d in order:
+        theirs = g_ref.at[1 - core, :, (p + 4 - d) % 4]
         remote(theirs, theirs, send.at[d], recv.at[d], sibling(p, q, x, core)).wait_recv()
     for cp in pending:
         cp.wait_send()
 
 
 def main_kernel(act_hbm, cot_hbm, w_hbm, coltab_hbm, rowtab_hbm, lw_ref, bias_ref,
-                dpre_hbm, s_ref, d_ref, g2_ref, lin_out_ref, imat_ref,
-                act, cot, w_ref, tab, dtab, syn, rowtab, rmat, lw_t, xs, rf, dpre, lin, t1, t2, g1, part,
+                dpre_hbm, s_ref, d_ref, rf2_ref, lin_out_ref,
+                act, cot, w_ref, tab, dtab, syn, rowtab, rmat, imat_ref, lw_t, bias_col, xs, rf, dpre, lin, t1, t2, g1, g2_ref, part,
                 b0, a1, b1, a2, b2, c0, e1, c1, e2, c2,
                 in_sem, out_sem, send1, recv1, send2, recv2, send3, recv3, send4, recv4, send5, recv5):
     p, q, x, core = place()
@@ -296,9 +314,14 @@
     rmat[:, :512] = kron8(rowtab[0], False)
     rmat[:, 512:] = kron8(rowtab[1], False)
     loads[0].wait()
-    for i in range(4):
-        loads[2 + i].wait()
-        columns(act[16 * i : 16 * i + 16], tab[...], xs, 16 * i, 16)
+
+    def analyse(i, _):
+        rows = pl.ds(16 * i, 16)
+        pltpu.make_async_copy(act_hbm.at[rows], act.at[rows], in_sem.at[2 + i]).wait()
+        columns(act[rows], tab[...], xs, pl.multiple_of(16 * i, 16), 16)
+        return 0
+
+    lax.fori_loop(0, 4, analyse, 0)
     row_modes(xs, rmat, t1, 1 - core)
     wait_peers()
     start_core(t1, b0, send1, recv1)
@@ -309,6 +332,7 @@
             imat_ref[:, :512] = kron8(rowtab[0], True)
             imat_ref[:, 512:] = kron8(rowtab[1], True)
             lw_t[...] = lw_ref[...].astype(F32).T.astype(BF)
+            bias_col[...] = jnp.broadcast_to(bias_ref[...], (128, 64)).T
         if i == 1:
             lane = lanes_of((512, 256)) % 128
             scaled = tab[...].astype(F32) * jnp.where(lane < 2, 2.0**-22, 2.0**-21)
@@ -328,28 +352,25 @@
 
     inverse(g1, imat_ref, rf)
     loads[7].wait()
-    bias = bias_ref[...]
 
     def rows(i, _):
+        bias = jnp.concatenate([bias_col[...]] * 4, axis=1)
         for n in range(2):
+            first = pl.multiple_of(16 * i + 8 * n, 8)
             ds = []
-            for k in range(2):
-                h = 4 * i + 2 * n + k
+            for k in range(8):
+                h = first + k
                 lhs = jnp.concatenate([rf[h], lw_t[...]], axis=1)
                 rhs = jnp.concatenate([syn[...], act[h]], axis=0)
                 d = (cot[h].astype(F32) * gelu_grad(dot(lhs, rhs) + bias)).astype(BF)
                 dpre[h] = d
                 ds.append(d)
-            columns(jnp.concatenate(ds, axis=0).reshape(2, 64, 512), dtab[...], xs, pl.multiple_of(4 * i + 2 * n, 2), 2)
+            columns(jnp.concatenate(ds, axis=0).reshape(8, 64, 512), dtab[...], xs, first, 8)
+        some = pl.ds(16 * i, 16)
+        pltpu.make_async_copy(dpre.at[some], dpre_hbm.at[some], out_sem.at[i]).start()
         return 0
 
-    stores = []
-    for i in range(4):
-        lax.fori_loop(4 * i, 4 * i + 4, rows, 0)
-        cp = pltpu.make_async_copy(dpre.at[pl.ds(16 * i, 16)], dpre_hbm.at[pl.ds(16 * i, 16)], out_sem.at[i])
-        cp.start()
-        stores.append(cp)
-
+    lax.fori_loop(0, 4, rows, 0)
     row_modes(xs, rmat, t2, 1 - core)
     start_core(t2, c0, send3, recv3)
     row_modes(xs, rmat, t2, core)
@@ -404,32 +425,55 @@
         g2_ref[core, p, q, x, g] = v.astype(BF)
     all_gather(g2_ref, send4, recv4, local_products)
     lin_out_ref[...] = join_lin(3) * (1.0 / 2048)
-    for cp in stores:
-        cp.wait()
-
-
-def last_kernel(g_ref, dpre_ref, imat_ref, coltab_hbm, lw_ref, s_ref, d_ref, gin_ref, gspec_ref, rf_ref, tab, ana, sem):
-    load = pltpu.make_async_copy(coltab_hbm.at[lax.axis_index("modes")], tab, sem)
+    inverse(g2_ref, imat_ref, rf2_ref)
+    for i in range(4):
+        some = pl.ds(16 * i, 16)
+        pltpu.make_async_copy(dpre.at[some], dpre_hbm.at[some], out_sem.at[i]).wait()
+
+
+def last_kernel(rf_hbm, dpre_hbm, coltab_hbm, lw_ref, s_ref, d_ref, lin_ref,
+                gin_hbm, gspec_hbm, glin_ref, gbias_ref, rf, dpre, tab, ana, gin, gspec, in_sem, out_sem):
+    load = pltpu.make_async_copy(coltab_hbm.at[lax.axis_index("modes")], tab, in_sem.at[8])
     load.start()
-    inverse(g_ref, imat_ref, rf_ref)
-    load.wait()
-    ana[...] = tab[:, :128].astype(F32).T.astype(BF)
-
-    def row(h, _):
-        for k in range(4):
-            lhs = jnp.concatenate([rf_ref[4 * h + k], lw_ref[...]], axis=1)
-            rhs = jnp.concatenate([ana[...], dpre_ref[4 * h + k]], axis=0)
-            gin_ref[4 * h + k] = dot(lhs, rhs).astype(BF)
-        return 0
-
-    lax.fori_loop(0, 16, row, 0)
+
+    def copy(n, i):
+        some = pl.ds(16 * i, 16)
+        if n == 2:
+            return pltpu.make_async_copy(gin.at[some], gin_hbm.at[some], out_sem.at[i])
+        src, dst = ((rf_hbm, rf), (dpre_hbm, dpre))[n]
+        return pltpu.make_async_copy(src.at[some], dst.at[some], in_sem.at[2 * i + n])
+
+    for i in range(4):
+        copy(0, i).start()
+        copy(1, i).start()
+    glin_ref[...] = lin_ref[:64]
+    gbias_ref[...] = lin_ref[64:65]
+    even = lax.broadcasted_iota(jnp.int32, (32, 64), 0) % 2 == 0
     for jj in range(2):
         re, im = duplicate(s_ref[jj])
         d = d_ref[jj]
-        even = lax.broadcasted_iota(jnp.int32, (32, 64), 0) % 2 == 0
         dsw = jnp.where(even, pltpu.roll(d, 31, 0), -pltpu.roll(d, 1, 0))
         for c in range(64):
-            gspec_ref[jj, c] = re[:, c : c + 1] * d + im[:, c : c + 1] * dsw
+            gspec[jj, c] = re[:, c : c + 1] * d + im[:, c : c + 1] * dsw
+        pltpu.make_async_copy(gspec.at[jj], gspec_hbm.at[jj], out_sem.at[4 + jj]).start()
+    load.wait()
+    ana[...] = tab[:, :128].astype(F32).T.astype(BF)
+
+    def row(i, _):
+        copy(0, i).wait()
+        copy(1, i).wait()
+        for k in range(16):
+            lhs = jnp.concatenate([rf[16 * i + k], lw_ref[...]], axis=1)
+            rhs = jnp.concatenate([ana[...], dpre[16 * i + k]], axis=0)
+            gin[16 * i + k] = dot(lhs, rhs).astype(BF)
+        copy(2, i).start()
+        return 0
+
+    lax.fori_loop(0, 4, row, 0)
+    for jj in range(2):
+        pltpu.make_async_copy(gspec.at[jj], gspec_hbm.at[jj], out_sem.at[4 + jj]).wait()
+    for i in range(4):
+        copy(2, i).wait()
 
 
 SPEC = (2, 4, 4, 4, 2, 16, 128)
@@ -444,32 +488,35 @@
     buffers = [pltpu.VMEM(quarter, BF), pltpu.VMEM(quarter, BF), pltpu.VMEM((3, 4, 4, 2, 16, 128), BF),
                pltpu.VMEM((4, 4, 2, 16, 128), BF), pltpu.VMEM((15, 2, 16, 128), BF)]
     shape = jax.ShapeDtypeStruct
-    dpre, s, d, g, lin, imat = pl.pallas_call(
+    dpre, s, d, rf, lin = pl.pallas_call(
         main_kernel,
-        out_shape=[shape((64, 64, 512), BF), shape((2, 32, 64), F32), shape((2, 32, 64), F32), shape(SPEC, BF),
-                   shape((80, 64), F32), shape((512, 1024), BF)],
+        out_shape=[shape((64, 64, 512), BF), shape((2, 32, 64), F32), shape((2, 32, 64), F32), shape((64, 64, 128), BF),
+                   shape((80, 64), F32)],
         in_specs=[ANY] * 5 + [VMEM] * 2,
-        out_specs=[ANY] + [VMEM] * 5,
+        out_specs=[ANY] + [VMEM] * 4,
         scratch_shapes=[
             pltpu.VMEM((64, 64, 512), BF), pltpu.VMEM((64, 64, 512), BF), pltpu.VMEM((2, 64, 32, 64), BF),
             pltpu.VMEM((512, 256), BF), pltpu.VMEM((512, 256), BF), pltpu.VMEM((128, 512), BF), pltpu.VMEM((2, 64, 64), BF),
-            pltpu.VMEM((512, 1024), BF), pltpu.VMEM((64, 64), BF), pltpu.VMEM((2, 1024, 512), BF),
+            pltpu.VMEM((512, 1024), BF), pltpu.VMEM((512, 1024), BF), pltpu.VMEM((64, 64), BF), pltpu.VMEM((64, 128), F32),
+            pltpu.VMEM((2, 1024, 512), BF),
             pltpu.VMEM((64, 64, 128), BF), pltpu.VMEM((64, 64, 512), BF), pltpu.VMEM((80, 64), F32),
-            pltpu.VMEM(SPEC, BF), pltpu.VMEM(SPEC, BF), pltpu.VMEM(SPEC, BF), pltpu.VMEM((4, 4, 80, 64), F32),
-        ] + buffers + buffers + [dma((8,)), dma((4,))] + [dma((22,))] * 8 + [dma((10,))] * 2,
+            pltpu.VMEM(SPEC, BF), pltpu.VMEM(SPEC, BF), pltpu.VMEM(SPEC, BF), pltpu.VMEM(SPEC, BF), pltpu.VMEM((4, 4, 80, 64), F32),
+        ] + buffers + buffers + [dma((8,)), dma((4,))] + [dma((31,))] * 8 + [dma((10,))] * 2,
         compiler_params=pltpu.CompilerParams(vmem_limit_bytes=LIMIT, collective_id=0, has_side_effects=True),
         name="main",
-    )(activations, cotangent, w, coltab, rowtab, linear_weight, bias[:, None])
-    gin, gspec = pl.pallas_call(
+    )(activations, cotangent, w, coltab, rowtab, linear_weight, bias.reshape(1, 64))
+    gin, gspec, glin, gbias = pl.pallas_call(
         last_kernel,
-        out_shape=[shape((64, 64, 512), BF), shape((2, 64, 32, 64), F32)],
-        in_specs=[VMEM] * 3 + [ANY] + [VMEM] * 3,
-        out_specs=[VMEM] * 2,
-        scratch_shapes=[pltpu.VMEM((64, 64, 128), BF), pltpu.VMEM((512, 256), BF), pltpu.VMEM((128, 512), BF), dma],
+        out_shape=[shape((64, 64, 512), BF), shape((2, 64, 32, 64), F32), shape((64, 64), F32), shape((1, 64), F32)],
+        in_specs=[ANY] * 3 + [VMEM] * 4,
+        out_specs=[ANY] * 2 + [VMEM] * 2,
+        scratch_shapes=[pltpu.VMEM((64, 64, 128), BF), pltpu.VMEM((64, 64, 512), BF), pltpu.VMEM((512, 256), BF),
+                        pltpu.VMEM((128, 512), BF), pltpu.VMEM((64, 64, 512), BF), pltpu.VMEM((2, 64, 32, 64), F32),
+                        dma((9,)), dma((6,))],
         compiler_params=pltpu.CompilerParams(vmem_limit_bytes=LIMIT),
         name="last",
-    )(g, dpre, imat, coltab, linear_weight, s, d)
-    return gin, gspec.transpose(0, 1, 3, 2), lin[:64], lin[64]
+    )(rf, dpre, coltab, linear_weight, s, d, lin)
+    return gin, gspec.transpose(0, 1, 3, 2), glin, gbias.reshape(64)
 
 
 def solution(mesh):

time: 102 us -> 87.5 us (0.86)
  Pallas kernels: 98.3 us -> 86.4 us
  local copies, waits for them, and re-layouts: 2.49 us -> 0 us
    pallas_call x1, Pallas kernels: 86 us -> 79.4 us  [body(): pl.pallas_call(main_kernel, out_shape=[shape((64, 64, 512), BF), shape((2...]
    pallas_call x1, Pallas kernels: 12.3 us -> 6.98 us  [body(): pl.pallas_call(last_kernel, out_shape=[shape((64, 64, 512), BF), shape((2...]
    broadcast_in_dim x1 -> x0, local copies, waits for them, and re-layouts: 1.36 us -> none  [body(): bias[:, None]]
where the time goes in v3:
time: 87.5 us; the launch traced here: 87.2 us
  Pallas kernels  86.4 us (99%)
    pallas_call x1, Pallas kernels, body(): pl.pallas_call(main_kernel, out_shape=[shape((64, 64, 512), BF), shape((2...  79.4 us
    pallas_call x1, Pallas kernels, body(): pl.pallas_call(last_kernel, out_shape=[shape((64, 64, 512), BF), shape((2...  6.98 us

profile of v3, /device:TPU:0, one launch (start us, length us, event | category | flops | bytes accessed | tf_op | source)
XLA Modules:
  0.0 87.2 jit_solution(17303633930323700437)
XLA Ops:
  0.6 79.4 %main.1 = (bf16[64,64,512]{2,1,0:T(8,128)(2,1)}, f32[2,32,64]{2,1,0:T(8,128)}, f32[2,32,64]{2,1,0:T(8,128)}, bf16[64,64,128]{2,1,0:T(8,128)(2,1)}, f32[80,64]{1,0:T(8,128)}) custom-call(bf16[64,64,512]{2,1,0:T(8,128)(2,1)} %act_hbm.1, bf16[64,64,512]{2,1,0:T(8,128)(2,1)} %cot_hbm.1, bf16[2,64,32,64]{3,2,1,0:T(8,128)(2,1)} %bitcast.4, ...), custom_call_target="tpu_custom_call" | custom-call | tf_op jit(solution)/shard_map/main/pallas_call | solution.py:491
  80.1 7.0 %last.1 = (bf16[64,64,512]{2,1,0:T(8,128)(2,1)}, f32[2,64,32,64]{3,2,1,0:T(8,128)}, f32[64,64]{1,0:T(8,128)}, f32[1,64]{1,0:T(1,128)}) custom-call(bf16[64,64,128]{2,1,0:T(8,128)(2,1)} %get-tuple-element.13.rf_hbm, bf16[64,64,512]{2,1,0:T(8,128)(2,1)} %get-tuple-element.14.dpre_hbm, bf16[4,512,256]{2,1,0:T(8,128)(2,1)} %constant.4.clone.coltab_hbm, ...), custom_call_target="tpu_custom_call" | custom-call | tf_op jit(solution)/shard_map/last/pallas_call | solution.py:508

commit v4 on v3

--- a/solution.py
+++ b/solution.py
@@ -44,9 +44,9 @@
 
 
 def kron8(table, flip):
-    up = (lax.broadcasted_iota(jnp.int32, (512, 64), 0) // 8 == lax.broadcasted_iota(jnp.int32, (512, 64), 1)).astype(BF)
-    wide = (lax.broadcasted_iota(jnp.int32, (64, 512), 1) // 8 == lax.broadcasted_iota(jnp.int32, (64, 512), 0)).astype(BF)
-    keep = lax.broadcasted_iota(jnp.int32, (512, 512), 0) % 8 == lax.broadcasted_iota(jnp.int32, (512, 512), 1) % 8
+    up = (lax.broadcasted_iota(jnp.int32, (512, 64), 0) >> 3 == lax.broadcasted_iota(jnp.int32, (512, 64), 1)).astype(BF)
+    wide = (lax.broadcasted_iota(jnp.int32, (64, 512), 1) >> 3 == lax.broadcasted_iota(jnp.int32, (64, 512), 0)).astype(BF)
+    keep = (lax.broadcasted_iota(jnp.int32, (512, 512), 0) ^ lax.broadcasted_iota(jnp.int32, (512, 512), 1)) & 7 == 0
     left = lax.dot_general(up, table, (((1,), (1 if flip else 0,)), ((), ())), preferred_element_type=F32).astype(BF)
     return jnp.where(keep, dot(left, wide), 0.0).astype(BF)
 
@@ -94,7 +94,7 @@
 
 
 def row_modes(xs_ref, rmat_ref, t_ref, owner):
-    block = lanes_of((256, 128)) // 32
+    block = lanes_of((256, 128)) >> 5
     for g in range(2):
         o = dot(rmat_ref[pl.ds(pl.multiple_of(owner * 256, 256), 256), :], xs_ref[g])
         for m in range(4):
@@ -110,9 +110,9 @@
                 t_ref[owner, m * (1 - owner) + z * owner, z * (1 - owner) + m * owner, :, g] = total[z]
 
 
-def inverse(g_ref, imat_ref, out_ref):
-    even = lanes_of((512, 128)) % 2 == 0
-    block = lanes_of((512, 128)) // 32
+def inverse(g_ref, imat_ref, out_ref, after=lambda b: None):
+    even = lanes_of((512, 128)) & 1 == 0
+    block = lanes_of((512, 128)) >> 5
     for b in range(4):
         cols = []
         for g in range(2):
@@ -130,6 +130,7 @@
         o = dot(imat_ref[...], jnp.concatenate(cols, axis=1))
         both = jnp.concatenate([o[:, :128].reshape(64, 8, 128), o[:, 128:].reshape(64, 8, 128)], axis=1)
         out_ref[:, 16 * b : 16 * b + 16, :] = both.astype(BF)
+        after(b)
 
 
 def gelu_grad(z):
@@ -142,7 +143,7 @@
 
 
 def duplicate(v):
-    even = lax.broadcasted_iota(jnp.int32, v.shape, 0) % 2 == 0
+    even = lax.broadcasted_iota(jnp.int32, v.shape, 0) & 1 == 0
     return jnp.where(even, v, pltpu.roll(v, 1, 0)), jnp.where(even, pltpu.roll(v, v.shape[0] - 1, 0), v)
 
 
@@ -156,7 +157,7 @@
 
 
 def to_block(cols):
-    block = lanes_of((8, 128)) // 32
+    block = lanes_of((8, 128)) >> 5
     parts = []
     for v in cols:
         square = jnp.concatenate([jnp.concatenate([v, v], axis=1)] * 4, axis=0).T
@@ -177,12 +178,12 @@
         w = w_ref[jj, c].astype(F32)
         t1 += re[:, c : c + 1] * w
         t2 += im[:, c : c + 1] * w
-    even = lax.broadcasted_iota(jnp.int32, (32, 64), 0) % 2 == 0
+    even = lax.broadcasted_iota(jnp.int32, (32, 64), 0) & 1 == 0
     return t1 + jnp.where(even, -pltpu.roll(t2, 31, 0), pltpu.roll(t2, 1, 0))
 
 
 def weigh_back(d, w_ref, jj):
-    even = lax.broadcasted_iota(jnp.int32, (32, 64), 0) % 2 == 0
+    even = lax.broadcasted_iota(jnp.int32, (32, 64), 0) & 1 == 0
     dsw = jnp.where(even, pltpu.roll(d, 31, 0), pltpu.roll(d, 1, 0))
     lane = lanes_of((32, 64))
     u1 = jnp.zeros((32, 64), F32)
@@ -194,107 +195,96 @@
     return jnp.where(even, u1 + pltpu.roll(u1, 31, 0), pltpu.roll(u2, 1, 0) - u2)
 
 
+FAR = (2, 1, 3, 0)
+NEAR = (0, 1, 3, 2)
+
+
+def arrived(ref, recv, k):
+    p, q, x, core = place()
+    remote(ref, ref, recv.at[k], recv.at[k], sibling(p, q, x, core)).wait_recv()
+
+
+def sent(ref, send, k):
+    p, q, x, core = place()
+    remote(ref, ref, send.at[k], send.at[k], sibling(p, q, x, core)).wait_send()
+
+
 def start_core(t_ref, b0, send, recv):
     p, q, x, core = place()
-    for d in (1, 2, 3, 0):
+    for d in FAR:
         row = (p + d) % 4
-        remote(t_ref.at[1 - core, :, row], b0.at[:, row], send.at[d], recv.at[d], sibling(p, q, x, core)).start()
+        remote(t_ref.at[1 - core, :, row], b0.at[:, row], send.at[0], recv.at[d], sibling(p, q, x, core)).start()
 
 
 def reduce_scatter(t_ref, bufs, send, recv, between=lambda i: None):
     b0, a1, b1, a2, b2 = bufs
     p, q, x, core = place()
-    pending = []
-    for d in (1, 2, 3, 0):
+    for d in FAR:
         row = (q + d) % 4
-        remote(b0.at[:, row], b0.at[:, row], send.at[d], recv.at[d], sibling(p, q, x, core)).wait_recv()
-        for e in (1, 2, 3, 0):
+        arrived(b0.at[:, row], recv, d)
+        for e in FAR:
             pt = (p + e) % 4
             a1[pt, row] = (t_ref[core, pt, row].astype(F32) + b0[pt, row].astype(F32)).astype(BF)
             if e:
-                k = 3 + 3 * d + e
-                cp = remote(a1.at[pt, row], b1.at[e - 1, row], send.at[k], recv.at[k], device(pt, q, x, core))
-                cp.start()
-                pending.append(cp)
+                remote(a1.at[pt, row], b1.at[e - 1, row], send.at[1], recv.at[4 + d], device(pt, q, x, core)).start()
     between(0)
-    stage = []
-    for i, d in enumerate((1, 2, 3, 0)):
+    for d in FAR:
         row = (q + d) % 4
-        for cp in pending[3 * i : 3 * i + 3]:
-            cp.wait_recv()
+        arrived(b1.at[:, row], recv, 4 + d)
         a2[row] = (a1[p, row].astype(F32) + b1[0, row].astype(F32) + b1[1, row].astype(F32) + b1[2, row].astype(F32)).astype(BF)
-        for n in range(4):
+        for n in FAR:
             k = 4 * d + n
             if k:
                 xt = (x + n) % 4
-                cp = remote(a2.at[row, xt], b2.at[k - 1], send.at[15 + k], recv.at[15 + k], device(p, row, xt, core))
-                cp.start()
-                stage.append(cp)
+                remote(a2.at[row, xt], b2.at[k - 1], send.at[2], recv.at[8], device(p, row, xt, core)).start()
     own = a1[p, q, x].astype(F32)
     for k in range(3):
         own += b1[k, q, x].astype(F32)
     between(1)
-    for cp in stage:
-        cp.wait_recv()
+    arrived(b2, recv, 8)
     for k in range(15):
         own += b2[k].astype(F32)
-    for d in range(4):
-        row = (p + d) % 4
-        remote(t_ref.at[1 - core, :, row], b0.at[:, row], send.at[d], recv.at[d], sibling(p, q, x, core)).wait_send()
-    for cp in pending + stage:
-        cp.wait_send()
     return own
 
 
+def drain_scatter(t_ref, bufs, send):
+    sent(t_ref.at[0], send, 0)
+    sent(bufs[2], send, 1)
+    sent(bufs[4], send, 2)
+
+
 def all_gather(g_ref, send, recv, between=lambda i: None):
     p, q, x, core = place()
-    pending = []
     mine = g_ref.at[core, p, q, x]
     for d in (0, 2, 1, 3):
-        for n in range(4):
-            k = 4 * d + n
-            if k:
-                cp = remote(mine, mine, send.at[15 + k], recv.at[15 + k], device(p, (q + d) % 4, (x + n) % 4, core))
-                cp.start()
-                pending.append(cp)
+        for n in FAR:
+            if 4 * d + n:
+                remote(mine, mine, send.at[2], recv.at[8 + d], device(p, (q + d) % 4, (x + n) % 4, core)).start()
     between(2)
-    order = (0, 1, 3, 2)
-    for d in order:
+    for d in NEAR:
         row = (q + 4 - d) % 4
-        for n in range(4):
-            k = 4 * d + n
-            if k:
-                xs = (x + 4 - n) % 4
-                theirs = g_ref.at[core, p, row, xs]
-                remote(theirs, theirs, send.at[15 + k], recv.at[15 + k], device(p, row, xs, core)).wait_recv()
+        arrived(g_ref.at[core, p, row, pl.ds(0, 4 if d else 3)], recv, 8 + d)
         mine = g_ref.at[core, p, row]
-        for e in (1, 2, 3):
-            k = 3 + 3 * d + e
-            cp = remote(mine, mine, send.at[k], recv.at[k], device((p + e) % 4, q, x, core))
-            cp.start()
-            pending.append(cp)
+        for e in (2, 1, 3):
+            remote(mine, mine, send.at[1], recv.at[4 + d], device((p + e) % 4, q, x, core)).start()
     between(3)
-    for d in order:
+    for d in NEAR:
         row = (q + 4 - d) % 4
-        for e in (1, 2, 3):
-            k = 3 + 3 * d + e
-            ps = (p + 4 - e) % 4
-            theirs = g_ref.at[core, ps, row]
-            remote(theirs, theirs, send.at[k], recv.at[k], device(ps, q, x, core)).wait_recv()
+        arrived(g_ref.at[core, pl.ds(0, 3), row], recv, 4 + d)
         theirs = g_ref.at[core, :, row]
-        cp = remote(theirs, theirs, send.at[d], recv.at[d], sibling(p, q, x, core))
-        cp.start()
-        pending.append(cp)
+        remote(theirs, theirs, send.at[0], recv.at[0], sibling(p, q, x, core)).start()
     between(4)
-    for d in order:
-        theirs = g_ref.at[1 - core, :, (p + 4 - d) % 4]
-        remote(theirs, theirs, send.at[d], recv.at[d], sibling(p, q, x, core)).wait_recv()
-    for cp in pending:
-        cp.wait_send()
+    arrived(g_ref.at[1 - core], recv, 0)
+
+
+def drain_gather(g_ref, bufs, send):
+    sent(g_ref.at[0], send, 0)
+    sent(g_ref.at[0, pl.ds(0, 3)], send, 1)
+    sent(bufs[4], send, 2)
 
 
 def main_kernel(act_hbm, cot_hbm, w_hbm, coltab_hbm, rowtab_hbm, lw_ref, bias_ref,
-                dpre_hbm, s_ref, d_ref, rf2_ref, lin_out_ref,
+                dpre_hbm, rf2_hbm, s_ref, d_ref, lin_out_ref,
                 act, cot, w_ref, tab, dtab, syn, rowtab, rmat, imat_ref, lw_t, bias_col, xs, rf, dpre, lin, t1, t2, g1, g2_ref, part,
                 b0, a1, b1, a2, b2, c0, e1, c1, e2, c2,
                 in_sem, out_sem, send1, recv1, send2, recv2, send3, recv3, send4, recv4, send5, recv5):
@@ -339,7 +329,8 @@
             dtab[...] = scaled.astype(BF)
             syn[...] = scaled[:, :128].T.astype(BF)
 
-    own = reduce_scatter(t1, (b0, a1, b1, a2, b2), send1, recv1, prepare)
+    first, second = (b0, a1, b1, a2, b2), (c0, e1, c1, e2, c2)
+    own = reduce_scatter(t1, first, send1, recv1, prepare)
     loads[6].wait()
     s = to_columns(own.astype(BF).astype(F32))
     mixed = []
@@ -348,7 +339,7 @@
         mixed.append(weigh(s[jj], w_ref, jj))
     for g, v in enumerate(to_block(mixed)):
         g1[core, p, q, x, g] = v.astype(BF)
-    all_gather(g1, send2, recv2)
+    all_gather(g1, send2, recv2, lambda i: drain_scatter(t1, first, send1) if i == 3 else None)
 
     inverse(g1, imat_ref, rf)
     loads[7].wait()
@@ -379,26 +370,24 @@
 
     def swap_lin():
         part[0, core] = lin[...]
+        drain_gather(g1, first, send2)
         remote(part.at[0, core], part.at[0, core], send5.at[0], recv5.at[0], sibling(p, q, x, core)).start()
 
     def join_lin(i):
         if i == 0:
-            cp = remote(part.at[0, core], part.at[0, core], send5.at[0], recv5.at[0], sibling(p, q, x, core))
-            cp.wait_send()
-            remote(part.at[0, 1 - core], part.at[0, 1 - core], send5.at[0], recv5.at[0], sibling(p, q, x, core)).wait_recv()
+            sent(part.at[0, 0], send5, 0)
+            arrived(part.at[0, 0], recv5, 0)
             return part[0, 0] + part[0, 1]
-        me, at = steps[i - 1]
-        for d in range(1, 4):
-            src = (me + 4 - d) % 4
-            remote(part.at[i, src], part.at[i, src], send5.at[3 * i - 3 + d], recv5.at[3 * i - 3 + d], at(src)).wait_recv()
-            remote(part.at[i, me], part.at[i, me], send5.at[3 * i - 3 + d], recv5.at[3 * i - 3 + d], at((me + d) % 4)).wait_send()
+        sent(part.at[i, pl.ds(0, 3)], send5, i)
+        arrived(part.at[i, pl.ds(0, 3)], recv5, i)
         return part[i, 0] + part[i, 1] + part[i, 2] + part[i, 3]
 
     def pass_lin(i):
         me, at = steps[i]
         part[i + 1, me] = join_lin(i)
+        mine = part.at[i + 1, me]
         for d in range(1, 4):
-            remote(part.at[i + 1, me], part.at[i + 1, me], send5.at[3 * i + d], recv5.at[3 * i + d], at((me + d) % 4)).start()
+            remote(mine, mine, send5.at[i + 1], recv5.at[i + 1], at((me + d) % 4)).start()
 
     def products(i, _):
         left = jnp.concatenate([act[4 * i + k] for k in range(4)], axis=1)
@@ -414,8 +403,10 @@
             swap_lin()
         if i >= 2:
             pass_lin(i - 2)
-
-    own = reduce_scatter(t2, (c0, e1, c1, e2, c2), send3, recv3, local_products)
+        if i == 3:
+            drain_scatter(t2, second, send3)
+
+    own = reduce_scatter(t2, second, send3, recv3, local_products)
     d = to_columns(own.astype(BF).astype(F32))
     back = []
     for jj in range(2):
@@ -424,11 +415,17 @@
     for g, v in enumerate(to_block(back)):
         g2_ref[core, p, q, x, g] = v.astype(BF)
     all_gather(g2_ref, send4, recv4, local_products)
+
+    def ship(b):
+        return pltpu.make_async_copy(rf.at[:, pl.ds(16 * b, 16)], rf2_hbm.at[:, pl.ds(16 * b, 16)], out_sem.at[4 + b])
+
+    inverse(g2_ref, imat_ref, rf, lambda b: ship(b).start())
     lin_out_ref[...] = join_lin(3) * (1.0 / 2048)
-    inverse(g2_ref, imat_ref, rf2_ref)
+    drain_gather(g2_ref, second, send4)
     for i in range(4):
         some = pl.ds(16 * i, 16)
         pltpu.make_async_copy(dpre.at[some], dpre_hbm.at[some], out_sem.at[i]).wait()
+        ship(i).wait()
 
 
 def last_kernel(rf_hbm, dpre_hbm, coltab_hbm, lw_ref, s_ref, d_ref, lin_ref,
@@ -448,7 +445,7 @@
         copy(1, i).start()
     glin_ref[...] = lin_ref[:64]
     gbias_ref[...] = lin_ref[64:65]
-    even = lax.broadcasted_iota(jnp.int32, (32, 64), 0) % 2 == 0
+    even = lax.broadcasted_iota(jnp.int32, (32, 64), 0) & 1 == 0
     for jj in range(2):
         re, im = duplicate(s_ref[jj])
         d = d_ref[jj]
@@ -488,12 +485,12 @@
     buffers = [pltpu.VMEM(quarter, BF), pltpu.VMEM(quarter, BF), pltpu.VMEM((3, 4, 4, 2, 16, 128), BF),
                pltpu.VMEM((4, 4, 2, 16, 128), BF), pltpu.VMEM((15, 2, 16, 128), BF)]
     shape = jax.ShapeDtypeStruct
-    dpre, s, d, rf, lin = pl.pallas_call(
+    dpre, rf, s, d, lin = pl.pallas_call(
         main_kernel,
-        out_shape=[shape((64, 64, 512), BF), shape((2, 32, 64), F32), shape((2, 32, 64), F32), shape((64, 64, 128), BF),
+        out_shape=[shape((64, 64, 512), BF), shape((64, 64, 128), BF), shape((2, 32, 64), F32), shape((2, 32, 64), F32),
                    shape((80, 64), F32)],
         in_specs=[ANY] * 5 + [VMEM] * 2,
-        out_specs=[ANY] + [VMEM] * 4,
+        out_specs=[ANY] * 2 + [VMEM] * 3,
         scratch_shapes=[
             pltpu.VMEM((64, 64, 512), BF), pltpu.VMEM((64, 64, 512), BF), pltpu.VMEM((2, 64, 32, 64), BF),
             pltpu.VMEM((512, 256), BF), pltpu.VMEM((512, 256), BF), pltpu.VMEM((128, 512), BF), pltpu.VMEM((2, 64, 64), BF),
@@ -501,7 +498,7 @@
             pltpu.VMEM((2, 1024, 512), BF),
             pltpu.VMEM((64, 64, 128), BF), pltpu.VMEM((64, 64, 512), BF), pltpu.VMEM((80, 64), F32),
             pltpu.VMEM(SPEC, BF), pltpu.VMEM(SPEC, BF), pltpu.VMEM(SPEC, BF), pltpu.VMEM(SPEC, BF), pltpu.VMEM((4, 4, 80, 64), F32),
-        ] + buffers + buffers + [dma((8,)), dma((4,))] + [dma((31,))] * 8 + [dma((10,))] * 2,
+        ] + buffers + buffers + [dma((8,)), dma((8,))] + [dma((3,)), dma((12,))] * 4 + [dma((4,))] * 2,
         compiler_params=pltpu.CompilerParams(vmem_limit_bytes=LIMIT, collective_id=0, has_side_effects=True),
         name="main",
     )(activations, cotangent, w, coltab, rowtab, linear_weight, bias.reshape(1, 64))

time: 87.5 us -> 82.9 us (0.947)
  Pallas kernels: 86.4 us -> 81.1 us
    pallas_call x1, Pallas kernels: 79.4 us -> 74.1 us  [body(): pl.pallas_call(main_kernel, out_shape=[shape((64, 64, 512), BF), shape((6...]
where the time goes in v4:
time: 82.9 us; the launch traced here: 81.9 us
  Pallas kernels  81.1 us (98%)
    pallas_call x1, Pallas kernels, body(): pl.pallas_call(main_kernel, out_shape=[shape((64, 64, 512), BF), shape((6...  74.1 us
    pallas_call x1, Pallas kernels, body(): pl.pallas_call(last_kernel, out_shape=[shape((64, 64, 512), BF), shape((2...  6.98 us

profile of v4, /device:TPU:0, one launch (start us, length us, event | category | flops | bytes accessed | tf_op | source)
XLA Modules:
  0.0 81.9 jit_solution(14385953747396273136)
XLA Ops:
  0.6 74.1 %main.1 = (bf16[64,64,512]{2,1,0:T(8,128)(2,1)}, bf16[64,64,128]{2,1,0:T(8,128)(2,1)}, f32[2,32,64]{2,1,0:T(8,128)}, f32[2,32,64]{2,1,0:T(8,128)}, f32[80,64]{1,0:T(8,128)}) custom-call(bf16[64,64,512]{2,1,0:T(8,128)(2,1)} %act_hbm.1, bf16[64,64,512]{2,1,0:T(8,128)(2,1)} %cot_hbm.1, bf16[2,64,32,64]{3,2,1,0:T(8,128)(2,1)} %bitcast.4, ...), custom_call_target="tpu_custom_call" | custom-call | tf_op jit(solution)/shard_map/main/pallas_call | solution.py:488
  74.7 7.0 %last.1 = (bf16[64,64,512]{2,1,0:T(8,128)(2,1)}, f32[2,64,32,64]{3,2,1,0:T(8,128)}, f32[64,64]{1,0:T(8,128)}, f32[1,64]{1,0:T(1,128)}) custom-call(bf16[64,64,128]{2,1,0:T(8,128)(2,1)} %get-tuple-element.13.rf_hbm, bf16[64,64,512]{2,1,0:T(8,128)(2,1)} %get-tuple-element.14.dpre_hbm, bf16[4,512,256]{2,1,0:T(8,128)(2,1)} %constant.4.clone.coltab_hbm, ...), custom_call_target="tpu_custom_call" | custom-call | tf_op jit(solution)/shard_map/last/pallas_call | solution.py:505

commit v5 on v4

--- a/solution.py
+++ b/solution.py
@@ -284,34 +284,38 @@
 
 
 def main_kernel(act_hbm, cot_hbm, w_hbm, coltab_hbm, rowtab_hbm, lw_ref, bias_ref,
-                dpre_hbm, rf2_hbm, s_ref, d_ref, lin_out_ref,
-                act, cot, w_ref, tab, dtab, syn, rowtab, rmat, imat_ref, lw_t, bias_col, xs, rf, dpre, lin, t1, t2, g1, g2_ref, part,
+                loc_hbm, rf2_hbm, s_ref, d_ref, lin_out_ref,
+                act, cot, w_ref, tab, dtab, syn, rowtab, rmat, imat_ref, lw_t, bias_col, xs, rf, dpre, loc, lin, t1, t2, g1, g2_ref, part,
                 b0, a1, b1, a2, b2, c0, e1, c1, e2, c2,
                 in_sem, out_sem, send1, recv1, send2, recv2, send3, recv3, send4, recv4, send5, recv5):
     p, q, x, core = place()
     signal_peers()
     row_dev, mode_dev = lax.axis_index("rows"), lax.axis_index("modes")
-    loads = [
-        pltpu.make_async_copy(coltab_hbm.at[mode_dev], tab, in_sem.at[0]),
-        pltpu.make_async_copy(rowtab_hbm.at[row_dev], rowtab, in_sem.at[1]),
-    ]
-    loads += [pltpu.make_async_copy(act_hbm.at[pl.ds(16 * i, 16)], act.at[pl.ds(16 * i, 16)], in_sem.at[2 + i]) for i in range(4)]
-    loads.append(pltpu.make_async_copy(w_hbm, w_ref, in_sem.at[6]))
-    loads.append(pltpu.make_async_copy(cot_hbm, cot, in_sem.at[7]))
-    for cp in loads:
-        cp.start()
-    loads[1].wait()
+    def load_act(i):
+        some = pl.ds(16 * i, 16)
+        return pltpu.make_async_copy(act_hbm.at[some], act.at[some], in_sem.at[2 + i])
+
+    load_rows = pltpu.make_async_copy(rowtab_hbm.at[row_dev], rowtab, in_sem.at[1])
+    load_cols = pltpu.make_async_copy(coltab_hbm.at[mode_dev], tab, in_sem.at[0])
+    load_w = pltpu.make_async_copy(w_hbm, w_ref, in_sem.at[6])
+    load_cot = pltpu.make_async_copy(cot_hbm, cot, in_sem.at[7])
+    load_rows.start()
+    load_cols.start()
+    for i in range(4):
+        load_act(i).start()
+    load_rows.wait()
     rmat[:, :512] = kron8(rowtab[0], False)
     rmat[:, 512:] = kron8(rowtab[1], False)
-    loads[0].wait()
+    load_cols.wait()
 
     def analyse(i, _):
-        rows = pl.ds(16 * i, 16)
-        pltpu.make_async_copy(act_hbm.at[rows], act.at[rows], in_sem.at[2 + i]).wait()
-        columns(act[rows], tab[...], xs, pl.multiple_of(16 * i, 16), 16)
+        load_act(i).wait()
+        columns(act[pl.ds(16 * i, 16)], tab[...], xs, pl.multiple_of(16 * i, 16), 16)
         return 0
 
     lax.fori_loop(0, 4, analyse, 0)
+    load_w.start()
+    load_cot.start()
     row_modes(xs, rmat, t1, 1 - core)
     wait_peers()
     start_core(t1, b0, send1, recv1)
@@ -331,7 +335,7 @@
 
     first, second = (b0, a1, b1, a2, b2), (c0, e1, c1, e2, c2)
     own = reduce_scatter(t1, first, send1, recv1, prepare)
-    loads[6].wait()
+    load_w.wait()
     s = to_columns(own.astype(BF).astype(F32))
     mixed = []
     for jj in range(2):
@@ -342,7 +346,7 @@
     all_gather(g1, send2, recv2, lambda i: drain_scatter(t1, first, send1) if i == 3 else None)
 
     inverse(g1, imat_ref, rf)
-    loads[7].wait()
+    load_cot.wait()
 
     def rows(i, _):
         bias = jnp.concatenate([bias_col[...]] * 4, axis=1)
@@ -357,8 +361,6 @@
                 dpre[h] = d
                 ds.append(d)
             columns(jnp.concatenate(ds, axis=0).reshape(8, 64, 512), dtab[...], xs, first, 8)
-        some = pl.ds(16 * i, 16)
-        pltpu.make_async_copy(dpre.at[some], dpre_hbm.at[some], out_sem.at[i]).start()
         return 0
 
     lax.fori_loop(0, 4, rows, 0)
@@ -405,6 +407,20 @@
             pass_lin(i - 2)
         if i == 3:
             drain_scatter(t2, second, send3)
+        if i in (1, 2):
+            lax.fori_loop(2 * i - 2, 2 * i, pointwise, 0)
+
+    def pointwise(i, _):
+        def some_rows(n, _):
+            for k in range(8):
+                h = 16 * i + 8 * n + k
+                loc[h] = dot(lw_ref[...], dpre[h]).astype(BF)
+            return 0
+
+        lax.fori_loop(0, 2, some_rows, 0)
+        some = pl.ds(16 * i, 16)
+        pltpu.make_async_copy(loc.at[some], loc_hbm.at[some], out_sem.at[i]).start()
+        return 0
 
     own = reduce_scatter(t2, second, send3, recv3, local_products)
     d = to_columns(own.astype(BF).astype(F32))
@@ -424,12 +440,12 @@
     drain_gather(g2_ref, second, send4)
     for i in range(4):
         some = pl.ds(16 * i, 16)
-        pltpu.make_async_copy(dpre.at[some], dpre_hbm.at[some], out_sem.at[i]).wait()
+        pltpu.make_async_copy(loc.at[some], loc_hbm.at[some], out_sem.at[i]).wait()
         ship(i).wait()
 
 
-def last_kernel(rf_hbm, dpre_hbm, coltab_hbm, lw_ref, s_ref, d_ref, lin_ref,
-                gin_hbm, gspec_hbm, glin_ref, gbias_ref, rf, dpre, tab, ana, gin, gspec, in_sem, out_sem):
+def last_kernel(rf_hbm, loc_hbm, coltab_hbm, s_ref, d_ref, lin_ref,
+                gin_hbm, gspec_hbm, glin_ref, gbias_ref, rf, loc, tab, ana, gin, gspec, in_sem, out_sem):
     load = pltpu.make_async_copy(coltab_hbm.at[lax.axis_index("modes")], tab, in_sem.at[8])
     load.start()
 
@@ -437,32 +453,41 @@
         some = pl.ds(16 * i, 16)
         if n == 2:
             return pltpu.make_async_copy(gin.at[some], gin_hbm.at[some], out_sem.at[i])
-        src, dst = ((rf_hbm, rf), (dpre_hbm, dpre))[n]
+        src, dst = ((rf_hbm, rf), (loc_hbm, loc))[n]
         return pltpu.make_async_copy(src.at[some], dst.at[some], in_sem.at[2 * i + n])
 
-    for i in range(4):
+    for i in range(2):
         copy(0, i).start()
         copy(1, i).start()
     glin_ref[...] = lin_ref[:64]
     gbias_ref[...] = lin_ref[64:65]
     even = lax.broadcasted_iota(jnp.int32, (32, 64), 0) & 1 == 0
-    for jj in range(2):
+    def products(jj, _):
         re, im = duplicate(s_ref[jj])
         d = d_ref[jj]
         dsw = jnp.where(even, pltpu.roll(d, 31, 0), -pltpu.roll(d, 1, 0))
         for c in range(64):
             gspec[jj, c] = re[:, c : c + 1] * d + im[:, c : c + 1] * dsw
         pltpu.make_async_copy(gspec.at[jj], gspec_hbm.at[jj], out_sem.at[4 + jj]).start()
+        return 0
+
+    lax.fori_loop(0, 2, products, 0)
     load.wait()
     ana[...] = tab[:, :128].astype(F32).T.astype(BF)
 
     def row(i, _):
         copy(0, i).wait()
         copy(1, i).wait()
-        for k in range(16):
-            lhs = jnp.concatenate([rf[16 * i + k], lw_ref[...]], axis=1)
-            rhs = jnp.concatenate([ana[...], dpre[16 * i + k]], axis=0)
-            gin[16 * i + k] = dot(lhs, rhs).astype(BF)
+
+        @pl.when(i < 2)
+        def _():
+            copy(0, i + 2).start()
+            copy(1, i + 2).start()
+
+        for k in range(4):
+            some = pl.ds(16 * i + 4 * k, 4)
+            part = dot(rf[some].reshape(256, 128), ana[...]).reshape(4, 64, 512)
+            gin[some] = (part + loc[some].astype(F32)).astype(BF)
         copy(2, i).start()
         return 0
 
@@ -485,7 +510,7 @@
     buffers = [pltpu.VMEM(quarter, BF), pltpu.VMEM(quarter, BF), pltpu.VMEM((3, 4, 4, 2, 16, 128), BF),
                pltpu.VMEM((4, 4, 2, 16, 128), BF), pltpu.VMEM((15, 2, 16, 128), BF)]
     shape = jax.ShapeDtypeStruct
-    dpre, rf, s, d, lin = pl.pallas_call(
+    loc, rf, s, d, lin = pl.pallas_call(
         main_kernel,
         out_shape=[shape((64, 64, 512), BF), shape((64, 64, 128), BF), shape((2, 32, 64), F32), shape((2, 32, 64), F32),
                    shape((80, 64), F32)],
@@ -496,7 +521,7 @@
             pltpu.VMEM((512, 256), BF), pltpu.VMEM((512, 256), BF), pltpu.VMEM((128, 512), BF), pltpu.VMEM((2, 64, 64), BF),
             pltpu.VMEM((512, 1024), BF), pltpu.VMEM((512, 1024), BF), pltpu.VMEM((64, 64), BF), pltpu.VMEM((64, 128), F32),
             pltpu.VMEM((2, 1024, 512), BF),
-            pltpu.VMEM((64, 64, 128), BF), pltpu.VMEM((64, 64, 512), BF), pltpu.VMEM((80, 64), F32),
+            pltpu.VMEM((64, 64, 128), BF), pltpu.VMEM((64, 64, 512), BF), pltpu.VMEM((64, 64, 512), BF), pltpu.VMEM((80, 64), F32),
             pltpu.VMEM(SPEC, BF), pltpu.VMEM(SPEC, BF), pltpu.VMEM(SPEC, BF), pltpu.VMEM(SPEC, BF), pltpu.VMEM((4, 4, 80, 64), F32),
         ] + buffers + buffers + [dma((8,)), dma((8,))] + [dma((3,)), dma((12,))] * 4 + [dma((4,))] * 2,
         compiler_params=pltpu.CompilerParams(vmem_limit_bytes=LIMIT, collective_id=0, has_side_effects=True),
@@ -505,14 +530,14 @@
     gin, gspec, glin, gbias = pl.pallas_call(
         last_kernel,
         out_shape=[shape((64, 64, 512), BF), shape((2, 64, 32, 64), F32), shape((64, 64), F32), shape((1, 64), F32)],
-        in_specs=[ANY] * 3 + [VMEM] * 4,
+        in_specs=[ANY] * 3 + [VMEM] * 3,
         out_specs=[ANY] * 2 + [VMEM] * 2,
         scratch_shapes=[pltpu.VMEM((64, 64, 128), BF), pltpu.VMEM((64, 64, 512), BF), pltpu.VMEM((512, 256), BF),
                         pltpu.VMEM((128, 512), BF), pltpu.VMEM((64, 64, 512), BF), pltpu.VMEM((2, 64, 32, 64), F32),
                         dma((9,)), dma((6,))],
         compiler_params=pltpu.CompilerParams(vmem_limit_bytes=LIMIT),
         name="last",
-    )(rf, dpre, coltab, linear_weight, s, d, lin)
+    )(rf, loc, coltab, s, d, lin)
     return gin, gspec.transpose(0, 1, 3, 2), glin, gbias.reshape(64)
 
 

time: 82.9 us -> 83.2 us (level)
  no operation moved by 1% of the time
where the time goes in v5:
time: 83.2 us; the launch traced here: 82.1 us
  Pallas kernels  81.3 us (98%)
    pallas_call x1, Pallas kernels, body(): pl.pallas_call(main_kernel, out_shape=[shape((64, 64, 512), BF), shape((6...  74.1 us
    pallas_call x1, Pallas kernels, body(): pl.pallas_call(last_kernel, out_shape=[shape((64, 64, 512), BF), shape((2...  7.24 us

profile of v5, /device:TPU:0, one launch (start us, length us, event | category | flops | bytes accessed | tf_op | source)
XLA Modules:
  0.0 82.1 jit_solution(18149406547519470391)
XLA Ops:
  0.6 74.1 %main.1 = (bf16[64,64,512]{2,1,0:T(8,128)(2,1)}, bf16[64,64,128]{2,1,0:T(8,128)(2,1)}, f32[2,32,64]{2,1,0:T(8,128)}, f32[2,32,64]{2,1,0:T(8,128)}, f32[80,64]{1,0:T(8,128)}) custom-call(bf16[64,64,512]{2,1,0:T(8,128)(2,1)} %act_hbm.1, bf16[64,64,512]{2,1,0:T(8,128)(2,1)} %cot_hbm.1, bf16[2,64,32,64]{3,2,1,0:T(8,128)(2,1)} %bitcast.4, ...), custom_call_target="tpu_custom_call" | custom-call | tf_op jit(solution)/shard_map/main/pallas_call | solution.py:513
  74.7 7.2 %last.1 = (bf16[64,64,512]{2,1,0:T(8,128)(2,1)}, f32[2,64,32,64]{3,2,1,0:T(8,128)}, f32[64,64]{1,0:T(8,128)}, f32[1,64]{1,0:T(1,128)}) custom-call(bf16[64,64,128]{2,1,0:T(8,128)(2,1)} %get-tuple-element.13.rf_hbm, bf16[64,64,512]{2,1,0:T(8,128)(2,1)} %get-tuple-element.14.loc_hbm, bf16[4,512,256]{2,1,0:T(8,128)(2,1)} %constant.4.clone.coltab_hbm, ...), custom_call_target="tpu_custom_call" | custom-call | tf_op jit(solution)/shard_map/last/pallas_call | solution.py:530

commit v6 on v5

--- a/solution.py
+++ b/solution.py
@@ -51,29 +51,29 @@
     return jnp.where(keep, dot(left, wide), 0.0).astype(BF)
 
 
-def place():
-    r, y = lax.axis_index("rows"), lax.axis_index("modes")
-    x, z, core = r // 8, (r // 2) % 4, r % 2
-    return y * (1 - core) + z * core, z * (1 - core) + y * core, x, core
-
-
-def device(p, q, x, core):
-    y, z = p * (1 - core) + q * core, q * (1 - core) + p * core
-    return ((x * 4 + z) * 2 + core, y)
-
-
-def sibling(p, q, x, core):
-    return device(q, p, x, 1 - core)
-
-
-def signal_peers():
-    p, q, x, core = place()
+class Spot:
+    def __init__(self):
+        r, y = lax.axis_index("rows"), lax.axis_index("modes")
+        x, z, core = lax.div(r, 8), lax.rem(lax.div(r, 2), 4), lax.rem(r, 2)
+        p, q = y * (1 - core) + z * core, z * (1 - core) + y * core
+        self.core, self.other = core, 1 - core
+        self.p = [lax.rem(p + d, 4) for d in range(4)]
+        self.q = [lax.rem(q + d, 4) for d in range(4)]
+        self.x = [lax.rem(x + d, 4) for d in range(4)]
+        self.sibling = (r + 1 - 2 * core, y)
+        self.first = [self.at(v, q, x) for v in self.p]
+        self.plane = [[self.at(p, v, u) for u in self.x] for v in self.q]
+
+    def at(self, p, q, x):
+        y, z = p * self.other + q * self.core, q * self.other + p * self.core
+        return ((x * 4 + z) * 2 + self.core, y)
+
+
+def signal_peers(spot):
     barrier = pltpu.get_barrier_semaphore()
-    pl.semaphore_signal(barrier, inc=1, device_id=sibling(p, q, x, core), device_id_type=MESH)
-    for d in range(1, 4):
-        pl.semaphore_signal(barrier, inc=1, device_id=device((p + d) % 4, q, x, core), device_id_type=MESH)
-    for k in range(1, 16):
-        pl.semaphore_signal(barrier, inc=1, device_id=device(p, (q + k // 4) % 4, (x + k % 4) % 4, core), device_id_type=MESH)
+    peers = [spot.sibling] + spot.first[1:] + [spot.plane[k // 4][k % 4] for k in range(1, 16)]
+    for peer in peers:
+        pl.semaphore_signal(barrier, inc=1, device_id=peer, device_id_type=MESH)
 
 
 def wait_peers():
@@ -199,88 +199,84 @@
 NEAR = (0, 1, 3, 2)
 
 
-def arrived(ref, recv, k):
-    p, q, x, core = place()
-    remote(ref, ref, recv.at[k], recv.at[k], sibling(p, q, x, core)).wait_recv()
-
-
-def sent(ref, send, k):
-    p, q, x, core = place()
-    remote(ref, ref, send.at[k], send.at[k], sibling(p, q, x, core)).wait_send()
-
-
-def start_core(t_ref, b0, send, recv):
-    p, q, x, core = place()
+def arrived(spot, ref, recv, k):
+    remote(ref, ref, recv.at[k], recv.at[k], spot.sibling).wait_recv()
+
+
+def sent(spot, ref, send, k):
+    remote(ref, ref, send.at[k], send.at[k], spot.sibling).wait_send()
+
+
+def start_core(spot, t_ref, b0, send, recv):
     for d in FAR:
-        row = (p + d) % 4
-        remote(t_ref.at[1 - core, :, row], b0.at[:, row], send.at[0], recv.at[d], sibling(p, q, x, core)).start()
-
-
-def reduce_scatter(t_ref, bufs, send, recv, between=lambda i: None):
+        row = spot.p[d]
+        remote(t_ref.at[spot.other, :, row], b0.at[:, row], send.at[0], recv.at[d], spot.sibling).start()
+
+
+def reduce_scatter(spot, t_ref, bufs, send, recv, between):
     b0, a1, b1, a2, b2 = bufs
-    p, q, x, core = place()
+    core, p, q, x = spot.core, spot.p[0], spot.q[0], spot.x[0]
     for d in FAR:
-        row = (q + d) % 4
-        arrived(b0.at[:, row], recv, d)
+        row = spot.q[d]
+        arrived(spot, b0.at[:, row], recv, d)
         for e in FAR:
-            pt = (p + e) % 4
+            pt = spot.p[e]
             a1[pt, row] = (t_ref[core, pt, row].astype(F32) + b0[pt, row].astype(F32)).astype(BF)
             if e:
-                remote(a1.at[pt, row], b1.at[e - 1, row], send.at[1], recv.at[4 + d], device(pt, q, x, core)).start()
+                remote(a1.at[pt, row], b1.at[e - 1, row], send.at[1], recv.at[4 + d], spot.first[e]).start()
     between(0)
     for d in FAR:
-        row = (q + d) % 4
-        arrived(b1.at[:, row], recv, 4 + d)
+        row = spot.q[d]
+        arrived(spot, b1.at[:, row], recv, 4 + d)
         a2[row] = (a1[p, row].astype(F32) + b1[0, row].astype(F32) + b1[1, row].astype(F32) + b1[2, row].astype(F32)).astype(BF)
         for n in FAR:
             k = 4 * d + n
             if k:
-                xt = (x + n) % 4
-                remote(a2.at[row, xt], b2.at[k - 1], send.at[2], recv.at[8], device(p, row, xt, core)).start()
+                remote(a2.at[row, spot.x[n]], b2.at[k - 1], send.at[2], recv.at[8], spot.plane[d][n]).start()
     own = a1[p, q, x].astype(F32)
     for k in range(3):
         own += b1[k, q, x].astype(F32)
     between(1)
-    arrived(b2, recv, 8)
+    arrived(spot, b2, recv, 8)
     for k in range(15):
         own += b2[k].astype(F32)
     return own
 
 
-def drain_scatter(t_ref, bufs, send):
-    sent(t_ref.at[0], send, 0)
-    sent(bufs[2], send, 1)
-    sent(bufs[4], send, 2)
-
-
-def all_gather(g_ref, send, recv, between=lambda i: None):
-    p, q, x, core = place()
-    mine = g_ref.at[core, p, q, x]
+def drain_scatter(spot, t_ref, bufs, send):
+    sent(spot, t_ref.at[0], send, 0)
+    sent(spot, bufs[2], send, 1)
+    sent(spot, bufs[4], send, 2)
+
+
+def all_gather(spot, g_ref, send, recv, between):
+    core, p = spot.core, spot.p[0]
+    mine = g_ref.at[core, p, spot.q[0], spot.x[0]]
     for d in (0, 2, 1, 3):
         for n in FAR:
             if 4 * d + n:
-                remote(mine, mine, send.at[2], recv.at[8 + d], device(p, (q + d) % 4, (x + n) % 4, core)).start()
+                remote(mine, mine, send.at[2], recv.at[8 + d], spot.plane[d][n]).start()
     between(2)
     for d in NEAR:
-        row = (q + 4 - d) % 4
-        arrived(g_ref.at[core, p, row, pl.ds(0, 4 if d else 3)], recv, 8 + d)
+        row = spot.q[(4 - d) % 4]
+        arrived(spot, g_ref.at[core, p, row, pl.ds(0, 4 if d else 3)], recv, 8 + d)
         mine = g_ref.at[core, p, row]
         for e in (2, 1, 3):
-            remote(mine, mine, send.at[1], recv.at[4 + d], device((p + e) % 4, q, x, core)).start()
+            remote(mine, mine, send.at[1], recv.at[4 + d], spot.first[e]).start()
     between(3)
     for d in NEAR:
-        row = (q + 4 - d) % 4
-        arrived(g_ref.at[core, pl.ds(0, 3), row], recv, 4 + d)
+        row = spot.q[(4 - d) % 4]
+        arrived(spot, g_ref.at[core, pl.ds(0, 3), row], recv, 4 + d)
         theirs = g_ref.at[core, :, row]
-        remote(theirs, theirs, send.at[0], recv.at[0], sibling(p, q, x, core)).start()
+        remote(theirs, theirs, send.at[0], recv.at[0], spot.sibling).start()
     between(4)
-    arrived(g_ref.at[1 - core], recv, 0)
-
-
-def drain_gather(g_ref, bufs, send):
-    sent(g_ref.at[0], send, 0)
-    sent(g_ref.at[0, pl.ds(0, 3)], send, 1)
-    sent(bufs[4], send, 2)
+    arrived(spot, g_ref.at[spot.other], recv, 0)
+
+
+def drain_gather(spot, g_ref, bufs, send):
+    sent(spot, g_ref.at[0], send, 0)
+    sent(spot, g_ref.at[0, pl.ds(0, 3)], send, 1)
+    sent(spot, bufs[4], send, 2)
 
 
 def main_kernel(act_hbm, cot_hbm, w_hbm, coltab_hbm, rowtab_hbm, lw_ref, bias_ref,
@@ -288,8 +284,9 @@
                 act, cot, w_ref, tab, dtab, syn, rowtab, rmat, imat_ref, lw_t, bias_col, xs, rf, dpre, loc, lin, t1, t2, g1, g2_ref, part,
                 b0, a1, b1, a2, b2, c0, e1, c1, e2, c2,
                 in_sem, out_sem, send1, recv1, send2, recv2, send3, recv3, send4, recv4, send5, recv5):
-    p, q, x, core = place()
-    signal_peers()
+    spot = Spot()
+    core, p, q, x = spot.core, spot.p[0], spot.q[0], spot.x[0]
+    signal_peers(spot)
     row_dev, mode_dev = lax.axis_index("rows"), lax.axis_index("modes")
     def load_act(i):
         some = pl.ds(16 * i, 16)
@@ -316,9 +313,9 @@
     lax.fori_loop(0, 4, analyse, 0)
     load_w.start()
     load_cot.start()
-    row_modes(xs, rmat, t1, 1 - core)
+    row_modes(xs, rmat, t1, spot.other)
     wait_peers()
-    start_core(t1, b0, send1, recv1)
+    start_core(spot, t1, b0, send1, recv1)
     row_modes(xs, rmat, t1, core)
 
     def prepare(i):
@@ -334,7 +331,7 @@
             syn[...] = scaled[:, :128].T.astype(BF)
 
     first, second = (b0, a1, b1, a2, b2), (c0, e1, c1, e2, c2)
-    own = reduce_scatter(t1, first, send1, recv1, prepare)
+    own = reduce_scatter(spot, t1, first, send1, recv1, prepare)
     load_w.wait()
     s = to_columns(own.astype(BF).astype(F32))
     mixed = []
@@ -343,7 +340,7 @@
         mixed.append(weigh(s[jj], w_ref, jj))
     for g, v in enumerate(to_block(mixed)):
         g1[core, p, q, x, g] = v.astype(BF)
-    all_gather(g1, send2, recv2, lambda i: drain_scatter(t1, first, send1) if i == 3 else None)
+    all_gather(spot, g1, send2, recv2, lambda i: drain_scatter(spot, t1, first, send1) if i == 3 else None)
 
     inverse(g1, imat_ref, rf)
     load_cot.wait()
@@ -364,32 +361,36 @@
         return 0
 
     lax.fori_loop(0, 4, rows, 0)
-    row_modes(xs, rmat, t2, 1 - core)
-    start_core(t2, c0, send3, recv3)
+    row_modes(xs, rmat, t2, spot.other)
+    start_core(spot, t2, c0, send3, recv3)
     row_modes(xs, rmat, t2, core)
 
-    steps = ((p, lambda v: device(v, q, x, core)), (q, lambda v: device(p, v, x, core)), (x, lambda v: device(p, q, v, core)))
+    steps = (
+        (p, spot.first[1:]),
+        (q, [spot.plane[d][0] for d in (1, 2, 3)]),
+        (x, [spot.plane[0][d] for d in (1, 2, 3)]),
+    )
 
     def swap_lin():
         part[0, core] = lin[...]
-        drain_gather(g1, first, send2)
-        remote(part.at[0, core], part.at[0, core], send5.at[0], recv5.at[0], sibling(p, q, x, core)).start()
+        drain_gather(spot, g1, first, send2)
+        remote(part.at[0, core], part.at[0, core], send5.at[0], recv5.at[0], spot.sibling).start()
 
     def join_lin(i):
         if i == 0:
-            sent(part.at[0, 0], send5, 0)
-            arrived(part.at[0, 0], recv5, 0)
+            sent(spot, part.at[0, 0], send5, 0)
+            arrived(spot, part.at[0, 0], recv5, 0)
             return part[0, 0] + part[0, 1]
-        sent(part.at[i, pl.ds(0, 3)], send5, i)
-        arrived(part.at[i, pl.ds(0, 3)], recv5, i)
+        sent(spot, part.at[i, pl.ds(0, 3)], send5, i)
+        arrived(spot, part.at[i, pl.ds(0, 3)], recv5, i)
         return part[i, 0] + part[i, 1] + part[i, 2] + part[i, 3]
 
     def pass_lin(i):
-        me, at = steps[i]
+        me, peers = steps[i]
         part[i + 1, me] = join_lin(i)
         mine = part.at[i + 1, me]
-        for d in range(1, 4):
-            remote(mine, mine, send5.at[i + 1], recv5.at[i + 1], at((me + d) % 4)).start()
+        for peer in peers:
+            remote(mine, mine, send5.at[i + 1], recv5.at[i + 1], peer).start()
 
     def products(i, _):
         left = jnp.concatenate([act[4 * i + k] for k in range(4)], axis=1)
@@ -401,14 +402,16 @@
     def local_products(i):
         if i == 0:
             lin[...] = jnp.zeros_like(lin)
-            lax.fori_loop(0, 16, products, 0)
+            lax.fori_loop(0, 8, products, 0)
+        if i == 1:
+            lax.fori_loop(8, 16, products, 0)
             swap_lin()
         if i >= 2:
             pass_lin(i - 2)
         if i == 3:
-            drain_scatter(t2, second, send3)
-        if i in (1, 2):
-            lax.fori_loop(2 * i - 2, 2 * i, pointwise, 0)
+            drain_scatter(spot, t2, second, send3)
+        if i in (2, 3):
+            lax.fori_loop(2 * i - 4, 2 * i - 2, pointwise, 0)
 
     def pointwise(i, _):
         def some_rows(n, _):
@@ -422,7 +425,7 @@
         pltpu.make_async_copy(loc.at[some], loc_hbm.at[some], out_sem.at[i]).start()
         return 0
 
-    own = reduce_scatter(t2, second, send3, recv3, local_products)
+    own = reduce_scatter(spot, t2, second, send3, recv3, local_products)
     d = to_columns(own.astype(BF).astype(F32))
     back = []
     for jj in range(2):
@@ -430,14 +433,14 @@
         back.append(weigh_back(d[jj], w_ref, jj))
     for g, v in enumerate(to_block(back)):
         g2_ref[core, p, q, x, g] = v.astype(BF)
-    all_gather(g2_ref, send4, recv4, local_products)
+    all_gather(spot, g2_ref, send4, recv4, local_products)
 
     def ship(b):
         return pltpu.make_async_copy(rf.at[:, pl.ds(16 * b, 16)], rf2_hbm.at[:, pl.ds(16 * b, 16)], out_sem.at[4 + b])
 
     inverse(g2_ref, imat_ref, rf, lambda b: ship(b).start())
     lin_out_ref[...] = join_lin(3) * (1.0 / 2048)
-    drain_gather(g2_ref, second, send4)
+    drain_gather(spot, g2_ref, second, send4)
     for i in range(4):
         some = pl.ds(16 * i, 16)
         pltpu.make_async_copy(loc.at[some], loc_hbm.at[some], out_sem.at[i]).wait()
@@ -456,7 +459,7 @@
         src, dst = ((rf_hbm, rf), (loc_hbm, loc))[n]
         return pltpu.make_async_copy(src.at[some], dst.at[some], in_sem.at[2 * i + n])
 
-    for i in range(2):
+    for i in range(4):
         copy(0, i).start()
         copy(1, i).start()
     glin_ref[...] = lin_ref[:64]
@@ -478,12 +481,6 @@
     def row(i, _):
         copy(0, i).wait()
         copy(1, i).wait()
-
-        @pl.when(i < 2)
-        def _():
-            copy(0, i + 2).start()
-            copy(1, i + 2).start()
-
         for k in range(4):
             some = pl.ds(16 * i + 4 * k, 4)
             part = dot(rf[some].reshape(256, 128), ana[...]).reshape(4, 64, 512)

time: 83.2 us -> 83 us (level)
  no operation moved by 1% of the time
where the time goes in v6:
time: 83 us; the launch traced here: 81.9 us
  Pallas kernels  81.1 us (98%)
    pallas_call x1, Pallas kernels, body(): pl.pallas_call(main_kernel, out_shape=[shape((64, 64, 512), BF), shape((6...  74 us
    pallas_call x1, Pallas kernels, body(): pl.pallas_call(last_kernel, out_shape=[shape((64, 64, 512), BF), shape((2...  7.05 us

profile of v6, /device:TPU:0, one launch (start us, length us, event | category | flops | bytes accessed | tf_op | source)
XLA Modules:
  0.0 81.9 jit_solution(9491323953974154797)
XLA Ops:
  0.6 74.0 %main.1 = (bf16[64,64,512]{2,1,0:T(8,128)(2,1)}, bf16[64,64,128]{2,1,0:T(8,128)(2,1)}, f32[2,32,64]{2,1,0:T(8,128)}, f32[2,32,64]{2,1,0:T(8,128)}, f32[80,64]{1,0:T(8,128)}) custom-call(bf16[64,64,512]{2,1,0:T(8,128)(2,1)} %act_hbm.1, bf16[64,64,512]{2,1,0:T(8,128)(2,1)} %cot_hbm.1, bf16[2,64,32,64]{3,2,1,0:T(8,128)(2,1)} %bitcast.4, ...), custom_call_target="tpu_custom_call" | custom-call | tf_op jit(solution)/shard_map/main/pallas_call | solution.py:510
  74.7 7.0 %last.1 = (bf16[64,64,512]{2,1,0:T(8,128)(2,1)}, f32[2,64,32,64]{3,2,1,0:T(8,128)}, f32[64,64]{1,0:T(8,128)}, f32[1,64]{1,0:T(1,128)}) custom-call(bf16[64,64,128]{2,1,0:T(8,128)(2,1)} %get-tuple-element.13.rf_hbm, bf16[64,64,512]{2,1,0:T(8,128)(2,1)} %get-tuple-element.14.loc_hbm, bf16[4,512,256]{2,1,0:T(8,128)(2,1)} %constant.4.clone.coltab_hbm, ...), custom_call_target="tpu_custom_call" | custom-call | tf_op jit(solution)/shard_map/last/pallas_call | solution.py:527

commit v7 on v6

--- a/solution.py
+++ b/solution.py
@@ -12,7 +12,6 @@
 BF = jnp.bfloat16
 F32 = jnp.float32
 VMEM = pl.BlockSpec(memory_space=pltpu.VMEM)
-LIMIT = 60 * 1024 * 1024
 
 
 def dot(a, b):
@@ -497,6 +496,7 @@
 
 SPEC = (2, 4, 4, 4, 2, 16, 128)
 ANY = pl.BlockSpec(memory_space=pl.ANY)
+HBM = pl.BlockSpec(memory_space=pltpu.HBM)
 
 
 def body(activations, cotangent, spectral_weight, linear_weight, bias):
@@ -511,7 +511,7 @@
         main_kernel,
         out_shape=[shape((64, 64, 512), BF), shape((64, 64, 128), BF), shape((2, 32, 64), F32), shape((2, 32, 64), F32),
                    shape((80, 64), F32)],
-        in_specs=[ANY] * 5 + [VMEM] * 2,
+        in_specs=[HBM] * 5 + [VMEM] * 2,
         out_specs=[ANY] * 2 + [VMEM] * 3,
         scratch_shapes=[
             pltpu.VMEM((64, 64, 512), BF), pltpu.VMEM((64, 64, 512), BF), pltpu.VMEM((2, 64, 32, 64), BF),
@@ -521,18 +521,18 @@
             pltpu.VMEM((64, 64, 128), BF), pltpu.VMEM((64, 64, 512), BF), pltpu.VMEM((64, 64, 512), BF), pltpu.VMEM((80, 64), F32),
             pltpu.VMEM(SPEC, BF), pltpu.VMEM(SPEC, BF), pltpu.VMEM(SPEC, BF), pltpu.VMEM(SPEC, BF), pltpu.VMEM((4, 4, 80, 64), F32),
         ] + buffers + buffers + [dma((8,)), dma((8,))] + [dma((3,)), dma((12,))] * 4 + [dma((4,))] * 2,
-        compiler_params=pltpu.CompilerParams(vmem_limit_bytes=LIMIT, collective_id=0, has_side_effects=True),
+        compiler_params=pltpu.CompilerParams(vmem_limit_bytes=44 * 1024 * 1024, collective_id=0, has_side_effects=True),
         name="main",
     )(activations, cotangent, w, coltab, rowtab, linear_weight, bias.reshape(1, 64))
     gin, gspec, glin, gbias = pl.pallas_call(
         last_kernel,
         out_shape=[shape((64, 64, 512), BF), shape((2, 64, 32, 64), F32), shape((64, 64), F32), shape((1, 64), F32)],
-        in_specs=[ANY] * 3 + [VMEM] * 3,
+        in_specs=[ANY] * 2 + [HBM] + [VMEM] * 3,
         out_specs=[ANY] * 2 + [VMEM] * 2,
         scratch_shapes=[pltpu.VMEM((64, 64, 128), BF), pltpu.VMEM((64, 64, 512), BF), pltpu.VMEM((512, 256), BF),
                         pltpu.VMEM((128, 512), BF), pltpu.VMEM((64, 64, 512), BF), pltpu.VMEM((2, 64, 32, 64), F32),
                         dma((9,)), dma((6,))],
-        compiler_params=pltpu.CompilerParams(vmem_limit_bytes=LIMIT),
+        compiler_params=pltpu.CompilerParams(vmem_limit_bytes=24 * 1024 * 1024),
         name="last",
     )(rf, loc, coltab, s, d, lin)
     return gin, gspec.transpose(0, 1, 3, 2), glin, gbias.reshape(64)

time: 83 us -> 85 us (1.024)
  local copies, waits for them, and re-layouts: 0 us -> 5.04 us
  Pallas kernels: 81.1 us -> 77.6 us
    unnamed x0 -> x10, local copies, waits for them, and re-layouts: none -> 5.04 us
    pallas_call x1, Pallas kernels: 7.05 us -> 5.32 us  [body(): pl.pallas_call(last_kernel, out_shape=[shape((64, 64, 512), BF), shape((2...]
    pallas_call x1, Pallas kernels: 74 us -> 72.3 us  [body(): pl.pallas_call(main_kernel, out_shape=[shape((64, 64, 512), BF), shape((6...]
where the time goes in v7:
time: 85 us; the launch traced here: 83.5 us
  Pallas kernels  77.6 us (91%)
  local copies, waits for them, and re-layouts  5.04 us (6%)
    pallas_call x1, Pallas kernels, body(): pl.pallas_call(main_kernel, out_shape=[shape((64, 64, 512), BF), shape((6...  72.3 us
    pallas_call x1, Pallas kernels, body(): pl.pallas_call(last_kernel, out_shape=[shape((64, 64, 512), BF), shape((2...  5.32 us
    unnamed x10, local copies, waits for them, and re-layouts  5.04 us

profile of v7, /device:TPU:0, one launch (start us, length us, event | category | flops | bytes accessed | tf_op | source)
XLA Modules:
  0.0 83.5 jit_solution(13620266596323659587)
XLA Ops:
  0.6 0.0 copy-start
  0.6 1.2 %copy-done = bf16[4,512,256]{2,1,0:T(8,128)(2,1)S(1)} copy-done((bf16[4,512,256]{2,1,0:T(8,128)(2,1)S(1)}, bf16[4,512,256]{2,1,0:T(8,128)(2,1)}, u32[]{:S(2)}) %copy-start) | copy-done | bytes 1048600
  1.9 0.0 copy-start.1
  1.9 1.2 %copy-done.1 = bf16[2,64,64,32]{2,3,1,0:T(8,128)(2,1)S(1)} copy-done((bf16[2,64,64,32]{2,3,1,0:T(8,128)(2,1)S(1)}, bf16[2,64,64,32]{2,3,1,0:T(8,128)(2,1)}, u32[]{:S(2)}) %copy-start.1) | copy-done | bytes 524312
  3.1 0.0 copy-start.2
  3.1 1.2 %copy-done.2 = bf16[32,2,64,64]{3,2,1,0:T(8,128)(2,1)S(1)} copy-done((bf16[32,2,64,64]{3,2,1,0:T(8,128)(2,1)S(1)}, bf16[32,2,64,64]{3,2,1,0:T(8,128)(2,1)}, u32[]{:S(2)}) %copy-start.2) | copy-done | bytes 524312
  4.3 0.0 copy-start.3
  4.3 0.7 copy-done.3
  5.0 0.0 copy-start.4
  5.0 0.7 copy-done.4
  5.7 72.3 %main.1 = (bf16[64,64,512]{2,1,0:T(8,128)(2,1)S(1)}, bf16[64,64,128]{2,1,0:T(8,128)(2,1)S(1)}, f32[2,32,64]{2,1,0:T(8,128)S(1)}, f32[2,32,64]{2,1,0:T(8,128)S(1)}, f32[80,64]{1,0:T(8,128)S(1)}) custom-call(bf16[64,64,512]{2,1,0:T(8,128)(2,1)} %act_hbm.1, bf16[64,64,512]{2,1,0:T(8,128)(2,1)} %cot_hbm.1, bf16[2,64,32,64]{3,2,1,0:T(8,128)(2,1)S(1)} %bitcast.4, ...), custom_call_target="tpu_custom_call" | custom-call | tf_op jit(solution)/shard_map/main/pallas_call | solution.py:510
  78.0 5.3 %last.1 = (bf16[64,64,512]{2,1,0:T(8,128)(2,1)}, f32[2,64,32,64]{3,2,1,0:T(8,128)}, f32[64,64]{1,0:T(8,128)}, f32[1,64]{1,0:T(1,128)}) custom-call(bf16[64,64,128]{2,1,0:T(8,128)(2,1)S(1)} %get-tuple-element.13.rf_hbm, bf16[64,64,512]{2,1,0:T(8,128)(2,1)S(1)} %get-tuple-element.14.loc_hbm, bf16[4,512,256]{2,1,0:T(8,128)(2,1)S(1)} %copy-done, ...), custom_call_target="tpu_custom_call" | custom-call | tf_op jit(solution)/shard_map/last/pallas_call | solution.py:527
Async XLA Ops:
  0.6 1.2 %copy-start = (bf16[4,512,256]{2,1,0:T(8,128)(2,1)S(1)}, bf16[4,512,256]{2,1,0:T(8,128)(2,1)}, u32[]{:S(2)}) copy-start(bf16[4,512,256]{2,1,0:T(8,128)(2,1)} %constant.4.clone.coltab_hbm) | copy-start | bytes 3145732
  1.9 1.2 %copy-start.1 = (bf16[2,64,64,32]{2,3,1,0:T(8,128)(2,1)S(1)}, bf16[2,64,64,32]{2,3,1,0:T(8,128)(2,1)}, u32[]{:S(2)}) copy-start(bf16[2,64,64,32]{2,3,1,0:T(8,128)(2,1)} %param.9) | copy-start | bytes 1572868
  3.1 1.2 %copy-start.2 = (bf16[32,2,64,64]{3,2,1,0:T(8,128)(2,1)S(1)}, bf16[32,2,64,64]{3,2,1,0:T(8,128)(2,1)}, u32[]{:S(2)}) copy-start(bf16[32,2,64,64]{3,2,1,0:T(8,128)(2,1)} %constant.5.clone.rowtab_hbm) | copy-start | bytes 1572868
  4.3 0.7 copy-start.3
  5.0 0.7 copy-start.4

commit v8 on v7

--- a/solution.py
+++ b/solution.py
@@ -278,9 +278,9 @@
     sent(spot, bufs[4], send, 2)
 
 
-def main_kernel(act_hbm, cot_hbm, w_hbm, coltab_hbm, rowtab_hbm, lw_ref, bias_ref,
+def main_kernel(act_hbm, cot_hbm, w_hbm, coltab_hbm, rowtab_hbm, lw_hbm, bias_hbm,
                 loc_hbm, rf2_hbm, s_ref, d_ref, lin_out_ref,
-                act, cot, w_ref, tab, dtab, syn, rowtab, rmat, imat_ref, lw_t, bias_col, xs, rf, dpre, loc, lin, t1, t2, g1, g2_ref, part,
+                lw_ref, bias_ref, act, cot, w_ref, tab, dtab, syn, rowtab, rmat, imat_ref, lw_t, bias_col, xs, rf, dpre, loc, lin, t1, t2, g1, g2_ref, part,
                 b0, a1, b1, a2, b2, c0, e1, c1, e2, c2,
                 in_sem, out_sem, send1, recv1, send2, recv2, send3, recv3, send4, recv4, send5, recv5):
     spot = Spot()
@@ -310,8 +310,10 @@
         return 0
 
     lax.fori_loop(0, 4, analyse, 0)
-    load_w.start()
-    load_cot.start()
+    load_lw = pltpu.make_async_copy(lw_hbm, lw_ref, in_sem.at[8])
+    load_bias = pltpu.make_async_copy(bias_hbm, bias_ref, in_sem.at[9])
+    for cp in (load_lw, load_bias, load_w, load_cot):
+        cp.start()
     row_modes(xs, rmat, t1, spot.other)
     wait_peers()
     start_core(spot, t1, b0, send1, recv1)
@@ -321,6 +323,8 @@
         if i == 0:
             imat_ref[:, :512] = kron8(rowtab[0], True)
             imat_ref[:, 512:] = kron8(rowtab[1], True)
+            load_lw.wait()
+            load_bias.wait()
             lw_t[...] = lw_ref[...].astype(F32).T.astype(BF)
             bias_col[...] = jnp.broadcast_to(bias_ref[...], (128, 64)).T
         if i == 1:
@@ -507,23 +511,25 @@
     buffers = [pltpu.VMEM(quarter, BF), pltpu.VMEM(quarter, BF), pltpu.VMEM((3, 4, 4, 2, 16, 128), BF),
                pltpu.VMEM((4, 4, 2, 16, 128), BF), pltpu.VMEM((15, 2, 16, 128), BF)]
     shape = jax.ShapeDtypeStruct
+    given = (activations, cotangent, w, coltab, rowtab, linear_weight, bias.reshape(1, 64))
     loc, rf, s, d, lin = pl.pallas_call(
         main_kernel,
         out_shape=[shape((64, 64, 512), BF), shape((64, 64, 128), BF), shape((2, 32, 64), F32), shape((2, 32, 64), F32),
                    shape((80, 64), F32)],
-        in_specs=[HBM] * 5 + [VMEM] * 2,
+        in_specs=[HBM] * 7,
         out_specs=[ANY] * 2 + [VMEM] * 3,
         scratch_shapes=[
+            pltpu.VMEM((64, 64), BF), pltpu.VMEM((1, 64), F32),
             pltpu.VMEM((64, 64, 512), BF), pltpu.VMEM((64, 64, 512), BF), pltpu.VMEM((2, 64, 32, 64), BF),
             pltpu.VMEM((512, 256), BF), pltpu.VMEM((512, 256), BF), pltpu.VMEM((128, 512), BF), pltpu.VMEM((2, 64, 64), BF),
             pltpu.VMEM((512, 1024), BF), pltpu.VMEM((512, 1024), BF), pltpu.VMEM((64, 64), BF), pltpu.VMEM((64, 128), F32),
             pltpu.VMEM((2, 1024, 512), BF),
             pltpu.VMEM((64, 64, 128), BF), pltpu.VMEM((64, 64, 512), BF), pltpu.VMEM((64, 64, 512), BF), pltpu.VMEM((80, 64), F32),
             pltpu.VMEM(SPEC, BF), pltpu.VMEM(SPEC, BF), pltpu.VMEM(SPEC, BF), pltpu.VMEM(SPEC, BF), pltpu.VMEM((4, 4, 80, 64), F32),
-        ] + buffers + buffers + [dma((8,)), dma((8,))] + [dma((3,)), dma((12,))] * 4 + [dma((4,))] * 2,
+        ] + buffers + buffers + [dma((10,)), dma((8,))] + [dma((3,)), dma((12,))] * 4 + [dma((4,))] * 2,
         compiler_params=pltpu.CompilerParams(vmem_limit_bytes=44 * 1024 * 1024, collective_id=0, has_side_effects=True),
         name="main",
-    )(activations, cotangent, w, coltab, rowtab, linear_weight, bias.reshape(1, 64))
+    )(*[pltpu.with_memory_space_constraint(v, pltpu.HBM) for v in given])
     gin, gspec, glin, gbias = pl.pallas_call(
         last_kernel,
         out_shape=[shape((64, 64, 512), BF), shape((2, 64, 32, 64), F32), shape((64, 64), F32), shape((1, 64), F32)],
@@ -534,7 +540,7 @@
                         dma((9,)), dma((6,))],
         compiler_params=pltpu.CompilerParams(vmem_limit_bytes=24 * 1024 * 1024),
         name="last",
-    )(rf, loc, coltab, s, d, lin)
+    )(rf, loc, pltpu.with_memory_space_constraint(coltab, pltpu.HBM), s, d, lin)
     return gin, gspec.transpose(0, 1, 3, 2), glin, gbias.reshape(64)
 
 

time: 85 us -> 80.4 us (0.946)
  local copies, waits for them, and re-layouts: 5.04 us -> 0 us
    unnamed x10 -> x0, local copies, waits for them, and re-layouts: 5.04 us -> none
where the time goes in v8:
time: 80.4 us; the launch traced here: 79 us
  Pallas kernels  78.2 us (97%)
    pallas_call x1, Pallas kernels, body(): pl.pallas_call(main_kernel, out_shape=[shape((64, 64, 512), BF), shape((6...  72.9 us
    pallas_call x1, Pallas kernels, body(): pl.pallas_call(last_kernel, out_shape=[shape((64, 64, 512), BF), shape((2...  5.3 us

profile of v8, /device:TPU:0, one launch (start us, length us, event | category | flops | bytes accessed | tf_op | source)
XLA Modules:
  0.0 79.0 jit_solution(11723273940943130794)
XLA Ops:
  0.6 72.9 %main.1 = (bf16[64,64,512]{2,1,0:T(8,128)(2,1)S(1)}, bf16[64,64,128]{2,1,0:T(8,128)(2,1)S(1)}, f32[2,32,64]{2,1,0:T(8,128)S(1)}, f32[2,32,64]{2,1,0:T(8,128)S(1)}, f32[80,64]{1,0:T(8,128)S(1)}) custom-call(bf16[64,64,512]{2,1,0:T(8,128)(2,1)} %act_hbm.1, bf16[64,64,512]{2,1,0:T(8,128)(2,1)} %cot_hbm.1, bf16[2,64,32,64]{3,2,1,0:T(8,128)(2,1)} %bitcast.4, ...), custom_call_target="tpu_custom_call" | custom-call | tf_op jit(solution)/shard_map/main/pallas_call | solution.py:515
  73.5 5.3 %last.1 = (bf16[64,64,512]{2,1,0:T(8,128)(2,1)}, f32[2,64,32,64]{3,2,1,0:T(8,128)}, f32[64,64]{1,0:T(8,128)}, f32[1,64]{1,0:T(1,128)}) custom-call(bf16[64,64,128]{2,1,0:T(8,128)(2,1)S(1)} %get-tuple-element.13.rf_hbm, bf16[64,64,512]{2,1,0:T(8,128)(2,1)S(1)} %get-tuple-element.14.loc_hbm, bf16[4,512,256]{2,1,0:T(8,128)(2,1)} %constant.4.clone.coltab_hbm, ...), custom_call_target="tpu_custom_call" | custom-call | tf_op jit(solution)/shard_map/last/pallas_call | solution.py:533
